TPU v7x, 32 devices: a whole 2x2x4 slice. The times are simulated.
32 devices in a mesh: rows: 16 (over z, y, core), cols: 2 (over x).
Axes of the slice: x: 2, y: 2, z: 4, core: 2. Of those that a mesh axis runs over, the one named last changes fastest.
Arguments:
- inputs: bfloat16 [96, 64, 640], P('rows', 'cols'), may hold values from -4 to 4
- qkv_weight: bfloat16 [640, 960], replicated, may hold values from -0.25 to 0.25
- out_weight: bfloat16 [320, 640], replicated, may hold values from -0.3125 to 0.3125
- attn_out: bfloat16 [96, 64, 320], P('rows', 'cols'), may hold values from -6 to 6
- log_norm: float32 [5, 96, 64], P(None, 'rows', 'cols'), may hold values from 4 to 6
- cotangent: bfloat16 [96, 64, 640], P('rows', 'cols'), may hold values from -6 to 6
Outputs:
- grad_input: bfloat16 [96, 64, 640], P('rows', 'cols')
- grad_qkv_weight: bfloat16 [640, 960], replicated
- grad_out_weight: bfloat16 [320, 640], replicated
All inputs are finite; a program needn't handle non-finite values.
Results may differ from a plain program's by a relative error of at most 0.01.
Values may be sent and summed in bfloat16 or wider, within the bound.
A program may use at most 64 MiB of HBM per device.

v0:
```python
import jax
import jax.numpy as jnp
from jax import lax
from jax.sharding import PartitionSpec as P

HEADS = 5
HEAD_DIM = 64
RADIUS = 6


def padded(block, sides, width):
    for axis, dim in sides:
        count = lax.axis_size(axis)
        forward = [(i, i + 1) for i in range(count - 1)]
        forward.append((count - 1, 0))
        backward = [(target, source) for source, target in forward]
        low = lax.ppermute(
            lax.slice_in_dim(block, block.shape[dim] - width, None, axis=dim), axis, forward
        )
        high = lax.ppermute(lax.slice_in_dim(block, 0, width, axis=dim), axis, backward)
        block = jnp.concatenate([low, block, high], axis=dim)
    return block


def window_mask(rows_dev, cols_dev, row_start, grid_rows):
    grown_cols = cols_dev + 2 * RADIUS
    grown_rows = rows_dev + 2 * RADIUS
    own_ids = jnp.arange(rows_dev * cols_dev)
    own_row = own_ids // cols_dev
    own_col = own_ids % cols_dev
    near_ids = jnp.arange(grown_rows * grown_cols)
    near_row = near_ids // grown_cols
    near_col = near_ids % grown_cols
    close_rows = jnp.abs(near_row[None, :] - RADIUS - own_row[:, None]) <= RADIUS
    close_cols = jnp.abs(near_col[None, :] - RADIUS - own_col[:, None]) <= RADIUS
    global_row = row_start + near_row - RADIUS
    in_grid = (global_row >= 0) & (global_row < grid_rows)
    return close_rows & close_cols & in_grid[None, :]


def shards(inputs, qkv_weight, out_weight, attn_out, log_norm, cotangent):
    rows_dev, cols_dev, model_width = inputs.shape
    tokens_dev = rows_dev * cols_dev
    inner_width = HEADS * HEAD_DIM
    score_scale = HEAD_DIM ** (-0.5)
    grown_rows = rows_dev + 2 * RADIUS
    grown_cols = cols_dev + 2 * RADIUS
    grown_tokens = grown_rows * grown_cols
    grid_tokens = tokens_dev * lax.axis_size("rows") * lax.axis_size("cols")
    grad_factor = grid_tokens ** (-0.5)
    flat_in = inputs.reshape(tokens_dev, model_width)
    flat_cot = cotangent.reshape(tokens_dev, model_width)
    flat_att = attn_out.reshape(tokens_dev, inner_width)
    projected = jnp.dot(flat_in, qkv_weight, preferred_element_type=jnp.float32).astype(
        jnp.bfloat16
    )
    grad_att = lax.dot_general(
        flat_cot, out_weight, (((1,), (1,)), ((), ())), preferred_element_type=jnp.float32
    ).astype(jnp.bfloat16)
    grad_wout = lax.dot_general(
        flat_att, flat_cot, (((0,), (0,)), ((), ())), preferred_element_type=jnp.float32
    )
    head_shape = (tokens_dev, HEADS, HEAD_DIM)
    queries = projected[:, :inner_width].reshape(head_shape)
    own_keyval = projected[:, inner_width:]
    upstream = grad_att.reshape(head_shape)
    row_delta = jnp.sum(
        upstream.astype(jnp.float32) * flat_att.reshape(head_shape).astype(jnp.float32), axis=2
    ).T
    own_norm = log_norm.reshape(HEADS, tokens_dev)
    inside = window_mask(
        rows_dev, cols_dev, lax.axis_index("rows") * rows_dev, rows_dev * lax.axis_size("rows")
    )
    block_keyval = own_keyval.reshape(rows_dev, cols_dev, 2 * inner_width)
    query_side = jnp.concatenate([projected[:, :inner_width], grad_att], axis=1).reshape(
        rows_dev, cols_dev, 2 * inner_width
    )
    near_keyval, near_qdo = (
        padded(block_keyval, (("rows", 0), ("cols", 1)), RADIUS),
        padded(query_side, (("rows", 0), ("cols", 1)), RADIUS),
    )
    own_stats = jnp.concatenate([own_norm, row_delta], axis=0).T.reshape(
        rows_dev, cols_dev, 2 * HEADS
    )
    near_stats = padded(own_stats, (("rows", 0), ("cols", 1)), RADIUS)
    flat_kv = near_keyval.reshape(grown_tokens, 2 * inner_width)
    near_keys = flat_kv[:, :inner_width].reshape(grown_tokens, HEADS, HEAD_DIM)
    near_values = flat_kv[:, inner_width:].reshape(grown_tokens, HEADS, HEAD_DIM)
    scores = (
        jnp.einsum("thd,ehd->hte", queries, near_keys, preferred_element_type=jnp.float32)
        * score_scale
    )
    weight = jnp.where(inside[None], jnp.exp(scores - own_norm[:, :, None]), 0.0)
    grad_weight = jnp.einsum(
        "thd,ehd->hte", upstream, near_values, preferred_element_type=jnp.float32
    )
    grad_score = (weight * (grad_weight - row_delta[:, :, None])).astype(jnp.bfloat16)
    grad_query = (
        jnp.einsum("hte,ehd->thd", grad_score, near_keys, preferred_element_type=jnp.float32)
        * score_scale
    )
    near_flat = near_qdo.reshape(grown_tokens, 2 * inner_width)
    near_queries = near_flat[:, :inner_width].reshape(grown_tokens, HEADS, HEAD_DIM)
    near_upstream = near_flat[:, inner_width:].reshape(grown_tokens, HEADS, HEAD_DIM)
    stats_flat = near_stats.reshape(grown_tokens, 2 * HEADS).T
    near_norm = stats_flat[:HEADS]
    near_delta = stats_flat[HEADS:]
    own_keys = own_keyval[:, :inner_width].reshape(head_shape)
    own_values = own_keyval[:, inner_width:].reshape(head_shape)
    scores_back = (
        jnp.einsum("ehd,thd->het", near_queries, own_keys, preferred_element_type=jnp.float32)
        * score_scale
    )
    weight_back = jnp.where(inside.T[None], jnp.exp(scores_back - near_norm[:, :, None]), 0.0)
    grad_back = jnp.einsum(
        "ehd,thd->het", near_upstream, own_values, preferred_element_type=jnp.float32
    )
    score_back_grad = (weight_back * (grad_back - near_delta[:, :, None])).astype(jnp.bfloat16)
    grad_keys = (
        jnp.einsum(
            "het,ehd->thd", score_back_grad, near_queries, preferred_element_type=jnp.float32
        )
        * score_scale
    )
    grad_values = jnp.einsum(
        "het,ehd->thd",
        weight_back.astype(jnp.bfloat16),
        near_upstream,
        preferred_element_type=jnp.float32,
    )
    grad_keyval = jnp.concatenate(
        [grad_keys.reshape(tokens_dev, inner_width), grad_values.reshape(tokens_dev, inner_width)],
        axis=1,
    )
    grad_proj = jnp.concatenate(
        [grad_query.reshape(tokens_dev, inner_width), grad_keyval], axis=1
    ).astype(jnp.bfloat16)
    grad_input = lax.dot_general(
        grad_proj, qkv_weight, (((1,), (1,)), ((), ())), preferred_element_type=jnp.float32
    ).astype(jnp.bfloat16)
    grad_input = grad_input.reshape(rows_dev, cols_dev, model_width)
    grad_wqkv = lax.dot_general(
        flat_in, grad_proj, (((0,), (0,)), ((), ())), preferred_element_type=jnp.float32
    )
    summed_wqkv, summed_wout = lax.psum((grad_wqkv, grad_wout), ("rows", "cols"))
    return (
        grad_input,
        (summed_wqkv * grad_factor).astype(jnp.bfloat16),
        (summed_wout * grad_factor).astype(jnp.bfloat16),
    )


def solution(mesh):
    in_specs = (
        P("rows", "cols", None),
        P(),
        P(),
        P("rows", "cols", None),
        P(None, "rows", "cols"),
        P("rows", "cols", None),
    )
    out_specs = (P("rows", "cols", None), P(), P())
    return jax.shard_map(shards, mesh=mesh, in_specs=in_specs, out_specs=out_specs, check_vma=False)
```

profile of v0, /device:TPU:0, one launch (start us, length us, event | category | flops | bytes accessed | tf_op | source)
XLA Modules:
  0.0 226.1 jit_solution(4671440812148472614)
XLA Ops:
  7.2 0.0 copy-start
  7.2 0.0 copy-start.19
  7.2 0.0 copy-start.25
  7.2 0.0 all-reduce.3.cloned.1.call-start
  7.3 1.2 copy-done
  8.5 1.5 convolution_convert_fusion
  10.0 0.8 fusion.37
  10.8 0.3 convolution_convert_fusion.2
  11.1 0.1 pad_maximum_fusion.3
  11.2 5.5 %collective-permute-start.5 = (bf16[6,32,640]{2,1,0:T(8,128)(2,1)S(1)}, bf16[6,32,640]{2,1,0:T(8,128)(2,1)S(1)}, u32[]{:S(2)}, u32[]{:S(2)}) collective-permute-start(bf16[6,32,640]{2,1,0:T(8,128)(2,1)S(1)} %bitcast.57), channel_id=1, source_target_pairs={{2,0},{4,2},{6,4},{8,6},{10,8},{12,10},{14,12},{16,14},{18,16},{20... | collective-permute-start | bytes 737288 | tf_op jit(solution)/shard_map/ppermute | solution.py:20
  16.7 0.1 copy.23
  16.9 0.1 reshape.292
  17.0 0.2 copy.25
  17.3 0.8 sub.133
  18.1 0.1 multiply_reduce_fusion
  18.2 0.1 reshape.285
  18.3 4.4 %collective-permute-start.9 = (f32[6,32,10]{1,0,2:T(8,128)S(1)}, f32[6,32,10]{1,0,2:T(8,128)S(1)}, u32[]{:S(2)}, u32[]{:S(2)}) collective-permute-start(f32[6,32,10]{1,0,2:T(8,128)S(1)} %reshape.285), channel_id=1, source_target_pairs={{2,0},{4,2},{6,4},{8,6},{10,8},{12,10},{14,12},{16,14},{18,16},{20... | collective-permute-start | bytes 23048 | tf_op jit(solution)/shard_map/ppermute | solution.py:20
  22.7 0.1 slice.67
  22.8 0.0 copy-start.3
  22.9 4.5 %collective-permute-start.1 = (bf16[6,32,640]{2,1,0:T(8,128)(2,1)S(1)}, bf16[6,32,640]{2,1,0:T(8,128)(2,1)S(1)}, u32[]{:S(2)}, u32[]{:S(2)}) collective-permute-start(bf16[6,32,640]{2,1,0:T(8,128)(2,1)S(1)} %bitcast.61), channel_id=1, source_target_pairs={{2,0},{4,2},{6,4},{8,6},{10,8},{12,10},{14,12},{16,14},{18,16},{20... | collective-permute-start | bytes 737288 | tf_op jit(solution)/shard_map/ppermute | solution.py:20
  27.4 1.1 fusion.16
  28.5 1.1 fusion.14
  29.6 0.1 fusion.38
  29.7 1.6 collective-permute-start.11
  31.2 0.5 collective-permute-start.10
  31.8 2.2 convolution_bitcast_fusion.1
  34.0 0.1 copy.22
  34.2 0.8 copy.27
  35.0 0.8 copy.29
  35.8 0.5 collective-permute-done.10
  36.3 1.1 pad_maximum_fusion.13
  37.3 0.1 reshape.286
  37.5 0.9 pad_maximum_fusion.8
  38.4 1.3 collective-permute-start.7
  39.7 0.8 collective-permute-start.6
  40.5 0.6 fusion.39
  41.1 3.0 %collective-permute-done = bf16[6,32,640]{2,1,0:T(8,128)(2,1)S(1)} collective-permute-done((bf16[6,32,640]{2,1,0:T(8,128)(2,1)S(1)}, bf16[6,32,640]{2,1,0:T(8,128)(2,1)S(1)}, u32[]{:S(2)}, u32[]{:S(2)}) %collective-permute-start) | collective-permute-done | bytes 245792 | tf_op jit(solution)/shard_map/ppermute | solution.py:17
  44.1 0.8 pad_maximum_fusion.11
  44.9 1.5 collective-permute-start.3
  46.4 0.5 collective-permute-start.2
  47.0 1.9 collective-permute-done.6
  48.8 1.4 pad_maximum_fusion.1
  50.2 0.2 reshape.282
  50.4 1.1 fusion.36
  51.5 2.2 copy.31
  53.7 1.1 copy.30
  54.8 1.5 pad_maximum_fusion
  56.3 0.2 reshape.274
  56.5 1.1 fusion.35
  57.6 1.4 copy.21
  59.1 1.1 copy.24
  60.2 0.7 fusion.41
  60.8 0.4 copy-done.16
  61.2 0.0 copy-done.21
  61.2 1.6 fusion.10
  62.8 4.3 %fusion.9 = bf16[5,64,192]{2,1,0:T(8,128)(2,1)} fusion(bf16[792,5,64]{0,2,1:T(8,128)(2,1)S(1)} %bitcast.54, f32[5,792,192]{1,2,0:T(8,128)} %copy-done.1, bf16[792,5,64]{0,2,1:T(8,128)(2,1)S(1)} %bitcast.72, bf16[192,5,64]{0,2,1:T(8,128)(2,1)S(1)} %bitcast.82, f32[5,792]{1,0:T(8,128)S(1)} %copy-done.26, f32[5,792]{1,0:T(8,128)S(1)} %copy-done.27, ...), kind=kOutput, calls=%fused_computation.16 | convolution fusion | flops 199326720 | bytes 4484544 | tf_op jit(solution)/shard_map/het,ehd->thd/dot_general | solution.py:120
  67.1 2.4 %fusion.40 = f32[5,192,792]{2,1,0:T(8,128)} fusion(bf16[192,5,64]{0,2,1:T(8,128)(2,1)S(1)} %bitcast.67, bf16[792,5,64]{0,2,1:T(8,128)(2,1)S(1)} %bitcast.55), kind=kOutput, calls=%fused_computation.77 | convolution fusion | flops 97320960 | bytes 3671040 | tf_op jit(solution)/shard_map/thd,ehd->hte/dot_general | solution.py:90
  69.5 3.8 %fusion.8 = bf16[5,64,192]{2,1,0:T(8,128)(2,1)S(1)} fusion(bf16[792,5,64]{0,2,1:T(8,128)(2,1)S(1)} %bitcast.56, f32[5,192,792]{2,1,0:T(8,128)} %fusion.40, bf16[192,5,64]{0,2,1:T(8,128)(2,1)S(1)} %bitcast.70, bf16[792,5,64]{0,2,1:T(8,128)(2,1)S(1)} %bitcast.73, f32[5,192]{1,0:T(8,128)S(1)} %bitcast.84, f32[5,192]{1,0:T(8,128)S(1)} %sub.133, ...), kind=kOutput, calls=%fused_computation.15 | convolution fusion | flops 199326720 | bytes 4460544 | tf_op jit(solution)/shard_map/hte,ehd->thd/dot_general | solution.py:99
  73.4 2.0 convolution_bitcast_fusion
  75.4 0.0 all-reduce.3.cloned.1.call-update
  75.4 1.2 convolution_convert_fusion.1
  76.6 138.8 %all-reduce.3.cloned.1.call-done = (f32[640,960]{0,1:T(8,128)}, f32[320,640]{1,0:T(8,128)}) async-done(((f32[640,960]{0,1:T(8,128)}, f32[320,640]{1,0:T(8,128)}), (f32[640,960]{0,1:T(8,128)}, f32[320,640]{1,0:T(8,128)})) %all-reduce.3.cloned.1.call-update) | async-done | bytes 3276816 | tf_op jit(solution)/shard_map/psum | solution.py:145
  215.4 3.0 %multiply_convert_fusion.2 = bf16[640,960]{0,1:T(8,128)(2,1)} fusion(f32[640,960]{0,1:T(8,128)} %get-tuple-element.3), kind=kLoop, calls=%fused_computation.4 | loop fusion | flops 1228800 | bytes 3686400 | tf_op jit(solution)/shard_map/convert_element_type | solution.py:148
  218.4 0.8 multiply_convert_fusion.3
  (66 shorter events, 0.2 us)
Async XLA Ops:
  7.2 1.3 copy-start
  7.2 3.6 %copy-start.19 = (bf16[6,32,640]{2,1,0:T(8,128)(2,1)S(1)}, bf16[6,32,640]{2,1,0:T(8,128)(2,1)}, u32[]{:S(2)}) copy-start(bf16[6,32,640]{2,1,0:T(8,128)(2,1)} %param.11) | copy-start | bytes 737284
  7.2 3.6 %copy-start.18 = (bf16[320,640]{1,0:T(8,128)(2,1)S(1)}, bf16[320,640]{1,0:T(8,128)(2,1)}, u32[]{:S(2)}) copy-start(bf16[320,640]{1,0:T(8,128)(2,1)} %param.8) | copy-start | bytes 1228804
  7.2 9.7 %copy-start.25 = (bf16[6,32,320]{2,1,0:T(8,128)(2,1)S(1)}, bf16[6,32,320]{2,1,0:T(8,128)(2,1)}, u32[]{:S(2)}) copy-start(bf16[6,32,320]{2,1,0:T(8,128)(2,1)} %param.9) | copy-start | bytes 368644
  7.2 208.2 %all-reduce.3.cloned.1.call-start = ((), (), s32[]{:S(2)}) async-start(), calls=%async_computation | async-start | bytes 6553600 | tf_op jit(solution)/shard_map/psum | solution.py:145
  11.2 26.2 %collective-permute-start.5 = (bf16[6,32,640]{2,1,0:T(8,128)(2,1)S(1)}, bf16[6,32,640]{2,1,0:T(8,128)(2,1)S(1)}, u32[]{:S(2)}, u32[]{:S(2)}) collective-permute-start(bf16[6,32,640]{2,1,0:T(8,128)(2,1)S(1)} %bitcast.57), channel_id=1, source_target_pairs={{2,0},{4,2},{6,4},{8,6},{10,8},{12,10},{14,12},{16,14},{18,16},{20... | collective-permute-start | bytes 737288 | tf_op jit(solution)/shard_map/ppermute | solution.py:20
  16.7 20.7 %collective-permute-start.4 = (bf16[6,32,640]{2,1,0:T(8,128)(2,1)S(1)}, bf16[6,32,640]{2,1,0:T(8,128)(2,1)}, u32[]{:S(2)}, u32[]{:S(2)}) collective-permute-start(bf16[6,32,640]{2,1,0:T(8,128)(2,1)S(1)} %bitcast.58), channel_id=1, source_target_pairs={{0,2},{2,4},{4,6},{6,8},{8,10},{10,12},{12,14},{14,16},{16,18},{18... | collective-permute-start | bytes 737288 | tf_op jit(solution)/shard_map/ppermute | solution.py:17
  16.9 14.9 %copy-start.12 = (bf16[192,320]{0,1:T(8,128)(2,1)}, bf16[192,320]{0,1:T(8,128)(2,1)S(1)}, u32[]{:S(2)}) copy-start(bf16[192,320]{0,1:T(8,128)(2,1)S(1)} %copy.23) | copy-start | bytes 368644
  18.1 16.0 %copy-start.15 = (bf16[192,320]{1,0:T(8,128)(2,1)S(1)}, bf16[192,320]{1,0:T(8,128)(2,1)}, u32[]{:S(2)}) copy-start(bf16[192,320]{1,0:T(8,128)(2,1)} %get-tuple-element.14) | copy-start | bytes 368644
  18.2 16.8 %copy-start.14 = (bf16[192,320]{1,0:T(8,128)(2,1)S(1)}, bf16[192,320]{1,0:T(8,128)(2,1)}, u32[]{:S(2)}) copy-start(bf16[192,320]{1,0:T(8,128)(2,1)} %get-tuple-element.13) | copy-start | bytes 368644
  18.3 11.3 %collective-permute-start.9 = (f32[6,32,10]{1,0,2:T(8,128)S(1)}, f32[6,32,10]{1,0,2:T(8,128)S(1)}, u32[]{:S(2)}, u32[]{:S(2)}) collective-permute-start(f32[6,32,10]{1,0,2:T(8,128)S(1)} %reshape.285), channel_id=1, source_target_pairs={{2,0},{4,2},{6,4},{8,6},{10,8},{12,10},{14,12},{16,14},{18,16},{20... | collective-permute-start | bytes 23048 | tf_op jit(solution)/shard_map/ppermute | solution.py:20
  22.7 6.9 %collective-permute-start.8 = (f32[6,32,10]{1,0,2:T(8,128)S(1)}, f32[6,32,10]{1,0,2:T(8,128)S(1)}, u32[]{:S(2)}, u32[]{:S(2)}) collective-permute-start(f32[6,32,10]{1,0,2:T(8,128)S(1)} %reshape.285), channel_id=1, source_target_pairs={{0,2},{2,4},{4,6},{6,8},{8,10},{10,12},{12,14},{14,16},{16,18},{18... | collective-permute-start | bytes 23048 | tf_op jit(solution)/shard_map/ppermute | solution.py:17
  22.8 21.3 %copy-start.3 = (bf16[192,640]{1,0:T(8,128)(2,1)}, bf16[192,640]{1,0:T(8,128)(2,1)S(1)}, u32[]{:S(2)}) copy-start(bf16[192,640]{1,0:T(8,128)(2,1)S(1)} %slice.67) | copy-start | bytes 737284
  22.9 18.2 %collective-permute-start.1 = (bf16[6,32,640]{2,1,0:T(8,128)(2,1)S(1)}, bf16[6,32,640]{2,1,0:T(8,128)(2,1)S(1)}, u32[]{:S(2)}, u32[]{:S(2)}) collective-permute-start(bf16[6,32,640]{2,1,0:T(8,128)(2,1)S(1)} %bitcast.61), channel_id=1, source_target_pairs={{2,0},{4,2},{6,4},{8,6},{10,8},{12,10},{14,12},{16,14},{18,16},{20... | collective-permute-start | bytes 737288 | tf_op jit(solution)/shard_map/ppermute | solution.py:20
  29.7 6.1 %collective-permute-start.11 = (f32[18,6,10]{1,0,2:T(8,128)S(1)}, f32[18,6,10]{1,0,2:T(8,128)S(1)}, u32[]{:S(2)}, u32[]{:S(2)}) collective-permute-start(f32[18,6,10]{1,0,2:T(8,128)S(1)} %get-tuple-element.17), channel_id=1, source_target_pairs={{1,0},{0,1},{3,2},{2,3},{5,4},{4,5},{7,6},{6,7},{9,8},{8,9},{11,10... | collective-permute-start | bytes 12968 | tf_op jit(solution)/shard_map/ppermute | solution.py:20
  31.2 5.0 %collective-permute-start.10 = (f32[18,6,10]{1,0,2:T(8,128)S(1)}, f32[18,6,10]{1,0,2:T(8,128)}, u32[]{:S(2)}, u32[]{:S(2)}) collective-permute-start(f32[18,6,10]{1,0,2:T(8,128)S(1)} %get-tuple-element.16), channel_id=1, source_target_pairs={{0,1},{1,0},{2,3},{3,2},{4,5},{5,4},{6,7},{7,6},{8,9},{9,8},{10,11... | collective-permute-start | bytes 12968 | tf_op jit(solution)/shard_map/ppermute | solution.py:17
  35.8 8.3 %collective-permute-start = (bf16[6,32,640]{2,1,0:T(8,128)(2,1)S(1)}, bf16[6,32,640]{2,1,0:T(8,128)(2,1)S(1)}, u32[]{:S(2)}, u32[]{:S(2)}) collective-permute-start(bf16[6,32,640]{2,1,0:T(8,128)(2,1)S(1)} %bitcast.62), channel_id=1, source_target_pairs={{0,2},{2,4},{4,6},{6,8},{8,10},{10,12},{12,14},{14,16},{16,18},{18... | collective-permute-start | bytes 737288 | tf_op jit(solution)/shard_map/ppermute | solution.py:17
  38.4 8.6 %collective-permute-start.7 = (bf16[18,6,640]{2,1,0:T(8,128)(2,1)S(1)}, bf16[18,6,640]{2,1,0:T(8,128)(2,1)S(1)}, u32[]{:S(2)}, u32[]{:S(2)}) collective-permute-start(bf16[18,6,640]{2,1,0:T(8,128)(2,1)S(1)} %get-tuple-element.12), channel_id=1, source_target_pairs={{1,0},{0,1},{3,2},{2,3},{5,4},{4,5},{7,6},{6,7},{9,8},{8,9},{11,10... | collective-permute-start | bytes 414728 | tf_op jit(solution)/shard_map/ppermute | solution.py:20
  39.7 9.1 %collective-permute-start.6 = (bf16[18,6,640]{2,1,0:T(8,128)(2,1)S(1)}, bf16[18,6,640]{2,1,0:T(8,128)(2,1)S(1)}, u32[]{:S(2)}, u32[]{:S(2)}) collective-permute-start(bf16[18,6,640]{2,1,0:T(8,128)(2,1)S(1)} %get-tuple-element.11), channel_id=1, source_target_pairs={{0,1},{1,0},{2,3},{3,2},{4,5},{5,4},{6,7},{7,6},{8,9},{9,8},{10,11... | collective-permute-start | bytes 414728 | tf_op jit(solution)/shard_map/ppermute | solution.py:17
  41.1 7.7 %copy-start.6 = (bf16[6,32,640]{2,1,0:T(8,128)(2,1)}, bf16[6,32,640]{2,1,0:T(8,128)(2,1)S(1)}, u32[]{:S(2)}) copy-start(bf16[6,32,640]{2,1,0:T(8,128)(2,1)S(1)} %collective-permute-done.1) | copy-start | bytes 737284
  44.1 2.9 %copy-start.8 = (bf16[6,32,640]{2,1,0:T(8,128)(2,1)}, bf16[6,32,640]{2,1,0:T(8,128)(2,1)S(1)}, u32[]{:S(2)}) copy-start(bf16[6,32,640]{2,1,0:T(8,128)(2,1)S(1)} %collective-permute-done) | copy-start | bytes 737284
  44.9 9.9 %collective-permute-start.3 = (bf16[18,6,640]{2,1,0:T(8,128)(2,1)}, bf16[18,6,640]{2,1,0:T(8,128)(2,1)}, u32[]{:S(2)}, u32[]{:S(2)}) collective-permute-start(bf16[18,6,640]{2,1,0:T(8,128)(2,1)} %get-tuple-element.10), channel_id=1, source_target_pairs={{1,0},{0,1},{3,2},{2,3},{5,4},{4,5},{7,6},{6,7},{9,8},{8,9},{11,10... | collective-permute-start | bytes 414728 | tf_op jit(solution)/shard_map/ppermute | solution.py:20
  46.4 8.4 %collective-permute-start.2 = (bf16[18,6,640]{2,1,0:T(8,128)(2,1)}, bf16[18,6,640]{2,1,0:T(8,128)(2,1)}, u32[]{:S(2)}, u32[]{:S(2)}) collective-permute-start(bf16[18,6,640]{2,1,0:T(8,128)(2,1)} %get-tuple-element.9), channel_id=1, source_target_pairs={{0,1},{1,0},{2,3},{3,2},{4,5},{5,4},{6,7},{7,6},{8,9},{9,8},{10,11... | collective-permute-start | bytes 414728 | tf_op jit(solution)/shard_map/ppermute | solution.py:17
  51.5 3.3 %copy-start.4 = (bf16[192,640]{1,0:T(8,128)(2,1)S(1)}, bf16[192,640]{1,0:T(8,128)(2,1)}, u32[]{:S(2)}) copy-start(bf16[192,640]{1,0:T(8,128)(2,1)} %copy-done.3) | copy-start | bytes 737284
  51.5 3.3 %copy-start.7 = (bf16[6,32,640]{2,1,0:T(8,128)(2,1)S(1)}, bf16[6,32,640]{2,1,0:T(8,128)(2,1)}, u32[]{:S(2)}) copy-start(bf16[6,32,640]{2,1,0:T(8,128)(2,1)} %copy-done.6) | copy-start | bytes 737284
  51.5 3.3 %copy-start.9 = (bf16[6,32,640]{2,1,0:T(8,128)(2,1)S(1)}, bf16[6,32,640]{2,1,0:T(8,128)(2,1)}, u32[]{:S(2)}) copy-start(bf16[6,32,640]{2,1,0:T(8,128)(2,1)} %copy-done.8) | copy-start | bytes 737284
  57.6 2.5 %copy-start.2 = (bf16[792,320]{0,1:T(8,128)(2,1)S(1)}, bf16[792,320]{0,1:T(8,128)(2,1)}, u32[]{:S(2)}) copy-start(bf16[792,320]{0,1:T(8,128)(2,1)} %copy.30) | copy-start | bytes 1520644
  57.6 2.5 %copy-start.11 = (bf16[192,320]{0,1:T(8,128)(2,1)S(1)}, bf16[192,320]{0,1:T(8,128)(2,1)}, u32[]{:S(2)}) copy-start(bf16[192,320]{0,1:T(8,128)(2,1)} %copy.27) | copy-start | bytes 368644
  60.1 1.1 copy-start.16
  60.1 1.1 copy-start.21
  60.1 1.1 copy-start.27
  60.8 2.0 copy-start.1
  61.2 1.6 copy-start.24
  61.2 1.6 copy-start.26
  67.1 2.4 %copy-start.13 = (bf16[192,320]{0,1:T(8,128)(2,1)S(1)}, bf16[192,320]{0,1:T(8,128)(2,1)}, u32[]{:S(2)}) copy-start(bf16[192,320]{0,1:T(8,128)(2,1)} %copy-done.12) | copy-start | bytes 368644
  67.1 2.4 %copy-start.17 = (bf16[792,320]{0,1:T(8,128)(2,1)S(1)}, bf16[792,320]{0,1:T(8,128)(2,1)}, u32[]{:S(2)}) copy-start(bf16[792,320]{0,1:T(8,128)(2,1)} %copy.24) | copy-start | bytes 1520644
  67.1 2.4 %copy-start.20 = (pred[192,792]{1,0:T(8,128)(4,1)S(1)}, pred[192,792]{1,0:T(8,128)(4,1)}, u32[]{:S(2)}) copy-start(pred[192,792]{1,0:T(8,128)(4,1)} %fusion.14) | copy-start | bytes 456196
  69.5 3.8 %copy-start.5 = (bf16[6,32,640]{2,1,0:T(8,128)(2,1)S(1)}, bf16[6,32,640]{2,1,0:T(8,128)(2,1)}, u32[]{:S(2)}) copy-start(bf16[6,32,640]{2,1,0:T(8,128)(2,1)} %param.6) | copy-start | bytes 737284
  69.5 3.8 %copy-start.22 = (bf16[5,64,192]{2,1,0:T(8,128)(2,1)S(1)}, bf16[5,64,192]{2,1,0:T(8,128)(2,1)}, u32[]{:S(2)}) copy-start(bf16[5,64,192]{2,1,0:T(8,128)(2,1)} %fusion.10) | copy-start | bytes 368644
  69.5 3.8 %copy-start.23 = (bf16[5,64,192]{2,1,0:T(8,128)(2,1)S(1)}, bf16[5,64,192]{2,1,0:T(8,128)(2,1)}, u32[]{:S(2)}) copy-start(bf16[5,64,192]{2,1,0:T(8,128)(2,1)} %fusion.9) | copy-start | bytes 368644
  215.4 3.0 %copy-start.10 = (f32[320,640]{1,0:T(8,128)S(1)}, f32[320,640]{1,0:T(8,128)}, u32[]{:S(2)}) copy-start(f32[320,640]{1,0:T(8,128)} %get-tuple-element.4) | copy-start | bytes 2457604
Sparse Core Ops, SparseCore 0:
  75.6 139.7 all-reduce.2
where the time goes:
time: 227 us; the launch traced here: 226 us
  waiting for transfers between devices  144 us (63%)
  starting transfers between devices  20.7 us (9%)
  matrix products  20 us (9%)
  local copies, waits for them, and re-layouts  14.9 us (7%)
  between operations  14.4 us (6%)
  other arithmetic  11.9 us (5%)
    psum x1, waiting for transfers between devices, shards(): lax.psum((grad_wqkv, grad_wout), ('rows', 'cols'))  139 us
    ppermute x6, starting transfers between devices, padded(): lax.ppermute(lax.slice_in_dim(block, 0, width, axis=dim), axis, backward)  18.8 us
    ppermute x6, waiting for transfers between devices, padded(): lax.ppermute(lax.slice_in_dim(block, block.shape[dim] - width, None, axis...  5.37 us
    unnamed x58, local copies, waits for them, and re-layouts  5.03 us
  transfers between devices with their start and end apart: 13, of which 4 were waited for; matrix products, arithmetic and copies ran while one was open for 8% of the time, Pallas kernels for 0%

commit v1 on v0

--- a/solution.py
+++ b/solution.py
@@ -1,11 +1,144 @@
+import functools
+
 import jax
 import jax.numpy as jnp
 from jax import lax
+from jax.experimental import pallas as pl
+from jax.experimental.pallas import tpu as pltpu
 from jax.sharding import PartitionSpec as P
 
 HEADS = 5
 HEAD_DIM = 64
 RADIUS = 6
+
+
+MESH = pl.DeviceIdType.MESH
+
+
+def reduce_kernel(
+    planes, depth, width, factor,
+    x_ref, o_ref, recv1, sum1, recv2, sum2, recv3,
+    s1, r1, s2, r2, s3, r3, zs, zr, ps, pr, cs, cr,
+):
+    row, col = lax.axis_index("rows"), lax.axis_index("cols")
+    core, lane, z = row % 2, (row // 2) % 2, row // 4
+    p = lane * width + col
+    partner = (row + 1 - 2 * core, col)
+
+    def plane_peer(k):
+        q = (p + k) % planes
+        return q, (z * 4 + (q // width) * 2 + core, q % width)
+
+    def z_peer(k):
+        q = (z + k) % depth
+        return q, (q * 4 + lane * 2 + core, col)
+
+    def send(src, dst, ssem, rsem, device):
+        copy = pltpu.make_async_remote_copy(
+            src_ref=src, dst_ref=dst, send_sem=ssem, recv_sem=rsem,
+            device_id=device, device_id_type=MESH,
+        )
+        copy.start()
+        return copy
+
+    barrier = pltpu.get_barrier_semaphore()
+    peers = [partner]
+    peers += [plane_peer(k)[1] for k in range(1, planes)]
+    peers += [z_peer(k)[1] for k in range(1, depth)]
+    for peer in peers:
+        pl.semaphore_signal(barrier, inc=1, device_id=peer, device_id_type=MESH)
+    pl.semaphore_wait(barrier, len(peers))
+
+    order = list(range(1, planes)) + [0]
+    pair, started = {}, []
+    for k in order:
+        q = (p + k) % planes
+        pair[k] = send(x_ref.at[1 - core, q], recv1.at[k], s1.at[k], r1.at[k], partner)
+    across = {}
+    for k in order:
+        q, device = plane_peer(k)
+        pair[k].wait_recv()
+        total = x_ref[core, q].astype(jnp.float32) + recv1[k].astype(jnp.float32)
+        sum1[k] = total.astype(jnp.bfloat16)
+        if k:
+            across[k] = send(sum1.at[k], recv2.at[k - 1], s2.at[k - 1], r2.at[k - 1], device)
+    total = sum1[0].astype(jnp.float32)
+    for k in range(1, planes):
+        across[k].wait_recv()
+        total = total + recv2[k - 1].astype(jnp.float32)
+    sum2[...] = total.astype(jnp.bfloat16)
+    deep = {}
+    for k in range(1, depth):
+        q, device = z_peer(k)
+        deep[k] = send(sum2.at[q], recv3.at[k - 1], s3.at[k - 1], r3.at[k - 1], device)
+    total = sum2[z].astype(jnp.float32)
+    for k in range(1, depth):
+        deep[k].wait_recv()
+        total = total + recv3[k - 1].astype(jnp.float32)
+    o_ref[core, p, z] = (total * factor).astype(jnp.bfloat16)
+
+    own = o_ref.at[core, p, z]
+    zcopies, pcopies = {}, {}
+    for k in range(1, depth):
+        zcopies[k] = send(own, own, zs.at[k - 1], zr.at[k - 1], z_peer(k)[1])
+
+    def share(kz, piece):
+        for k in range(1, planes):
+            pcopies[k, kz] = send(
+                piece, piece, ps.at[k - 1, kz], pr.at[k - 1, kz], plane_peer(k)[1]
+            )
+        started.append(send(piece, piece, cs.at[0, kz], cr.at[0, kz], partner))
+
+    share(0, own)
+    for k in range(1, depth):
+        zcopies[k].wait_recv()
+        share(k, o_ref.at[core, p, (z - k + depth) % depth])
+    for kz in range(depth):
+        for k in range(1, planes):
+            pcopies[k, kz].wait_recv()
+            piece = o_ref.at[core, (p - k + planes) % planes, (z - kz + depth) % depth]
+            started.append(send(piece, piece, cs.at[k, kz], cr.at[k, kz], partner))
+    for copy in started:
+        copy.wait_recv()
+    for copy in [*started, *pair.values(), *across.values(), *deep.values(),
+                 *zcopies.values(), *pcopies.values()]:
+        copy.wait_send()
+
+
+def summed(parts, factor):
+    rows = parts.shape[0]
+    columns = parts.shape[1]
+    count, width = lax.axis_size("rows"), lax.axis_size("cols")
+    planes, depth = 2 * width, max(count // 4, 1)
+    half = columns // 2
+    if count % 4 or rows % (planes * depth * 8) or columns % 256 or depth < 2:
+        return (lax.psum(parts, ("rows", "cols")) * factor).astype(jnp.bfloat16)
+    high = rows // (planes * depth)
+    x = parts.astype(jnp.bfloat16).reshape(planes, depth, high, 2, half).transpose(3, 0, 1, 2, 4)
+    low = jnp.bfloat16
+    dma = pltpu.SemaphoreType.DMA
+    out = pl.pallas_call(
+        functools.partial(reduce_kernel, planes, depth, width, factor),
+        out_shape=jax.ShapeDtypeStruct((2, planes, depth, high, half), low),
+        in_specs=[pl.BlockSpec(memory_space=pltpu.VMEM)],
+        out_specs=pl.BlockSpec(memory_space=pltpu.VMEM),
+        scratch_shapes=[
+            pltpu.VMEM((planes, depth, high, half), low),
+            pltpu.VMEM((planes, depth, high, half), low),
+            pltpu.VMEM((planes - 1, depth, high, half), low),
+            pltpu.VMEM((depth, high, half), low),
+            pltpu.VMEM((depth - 1, high, half), low),
+            dma((planes,)), dma((planes,)),
+            dma((planes - 1,)), dma((planes - 1,)),
+            dma((depth - 1,)), dma((depth - 1,)),
+            dma((depth - 1,)), dma((depth - 1,)),
+            dma((planes - 1, depth)), dma((planes - 1, depth)),
+            dma((planes, depth)), dma((planes, depth)),
+        ],
+        compiler_params=pltpu.CompilerParams(collective_id=0, has_side_effects=True),
+        name="weight_sums",
+    )(x)
+    return out.transpose(1, 2, 3, 0, 4).reshape(rows, columns)
 
 
 def padded(block, sides, width):
@@ -58,7 +191,7 @@
         flat_cot, out_weight, (((1,), (1,)), ((), ())), preferred_element_type=jnp.float32
     ).astype(jnp.bfloat16)
     grad_wout = lax.dot_general(
-        flat_att, flat_cot, (((0,), (0,)), ((), ())), preferred_element_type=jnp.float32
+        flat_cot, flat_att, (((0,), (0,)), ((), ())), preferred_element_type=jnp.float32
     )
     head_shape = (tokens_dev, HEADS, HEAD_DIM)
     queries = projected[:, :inner_width].reshape(head_shape)
@@ -142,12 +275,9 @@
     grad_wqkv = lax.dot_general(
         flat_in, grad_proj, (((0,), (0,)), ((), ())), preferred_element_type=jnp.float32
     )
-    summed_wqkv, summed_wout = lax.psum((grad_wqkv, grad_wout), ("rows", "cols"))
-    return (
-        grad_input,
-        (summed_wqkv * grad_factor).astype(jnp.bfloat16),
-        (summed_wout * grad_factor).astype(jnp.bfloat16),
-    )
+    sums = summed(jnp.concatenate([grad_wqkv, grad_wout], axis=1), grad_factor)
+    columns = grad_wqkv.shape[1]
+    return grad_input, sums[:, :columns], sums[:, columns:].T
 
 
 def solution(mesh):

time: 227 us -> 118 us (0.52)
  waiting for transfers between devices: 144 us -> 6.56 us
  Pallas kernels: 0 us -> 35.2 us
  local copies, waits for them, and re-layouts: 14.9 us -> 28.5 us
  between operations: 14.4 us -> 1.04 us
  other arithmetic: 11.9 us -> 7.46 us
    psum x1 -> x0, waiting for transfers between devices: 139 us -> none  [shards(): lax.psum((grad_wqkv, grad_wout), ('rows', 'cols'))]
    pallas_call x0 -> x1, Pallas kernels: none -> 35.2 us  [summed(): pl.pallas_call(functools.partial(reduce_kernel, planes, depth, width, fac...]
    convert_element_type x0 -> x2, local copies, waits for them, and re-layouts: none -> 4.9 us  [summed(): parts.astype(jnp.bfloat16).reshape(planes, depth, high, 2, half)]
    convert_element_type x2 -> x0, other arithmetic: 3.85 us -> none  [the longest x1 3.02 us: shards(): (summed_wqkv * grad_factor).astype(jnp.bfloat16)]
    transpose x0 -> x2, local copies, waits for them, and re-layouts: none -> 3.34 us  [the longest x1 3.12 us: summed(): return out.transpose(1, 2, 3, 0, 4).reshape(rows, columns)]
    unnamed x58 -> x61, local copies, waits for them, and re-layouts: 5.03 us -> 7.7 us
    concatenate x0 -> x1, local copies, waits for them, and re-layouts: none -> 2.46 us  [shards(): sums = summed(jnp.concatenate([grad_wqkv, grad_wout], axis=1), grad_factor)]
  transfers between devices with their start and end apart: 13 -> 12, of which waited for: 4 -> 5; matrix products, arithmetic and copies ran while one was open for 8% -> 14% of each run, Pallas kernels for 0% -> 0%
where the time goes in v1:
time: 118 us
  Pallas kernels  35.2 us (30%)
  local copies, waits for them, and re-layouts  28.5 us (24%)
  starting transfers between devices  20.7 us (18%)
  matrix products  18.3 us (16%)
  other arithmetic  7.46 us (6%)
  waiting for transfers between devices  6.56 us (6%)
    pallas_call x1, Pallas kernels, summed(): pl.pallas_call(functools.partial(reduce_kernel, planes, depth, width, fac...  35.2 us
    ppermute x6, starting transfers between devices, padded(): lax.ppermute(lax.slice_in_dim(block, 0, width, axis=dim), axis, backward)  18.7 us
    unnamed x61, local copies, waits for them, and re-layouts  7.7 us
    ppermute x6, waiting for transfers between devices, padded(): lax.ppermute(lax.slice_in_dim(block, block.shape[dim] - width, None, axis...  6.31 us
    convert_element_type x2, local copies, waits for them, and re-layouts, summed(): parts.astype(jnp.bfloat16).reshape(planes, depth, high, 2, half)  4.9 us
    dot_general x1, matrix products, shards(): jnp.einsum('het,ehd->thd', score_back_grad, near_queries, preferred_eleme...  4.31 us
    dot_general x1, matrix products, shards(): jnp.einsum('hte,ehd->thd', grad_score, near_keys, preferred_element_type=...  3.8 us
    concatenate x4, other arithmetic, padded(): block = jnp.concatenate([low, block, high], axis=dim)  3.17 us
  transfers between devices with their start and end apart: 12, of which 5 were waited for; matrix products, arithmetic and copies ran while one was open for 14% of the time, Pallas kernels for 0%

profile of v1, /device:TPU:0, one launch (start us, length us, event | category | flops | bytes accessed | tf_op | source)
XLA Modules:
  0.0 117.7 jit_solution(12986845191739320018)
XLA Ops:
  0.7 1.2 %copy-done = bf16[640,960]{0,1:T(8,128)(2,1)S(1)} copy-done((bf16[640,960]{0,1:T(8,128)(2,1)S(1)}, bf16[640,960]{0,1:T(8,128)(2,1)}, u32[]{:S(2)}) %copy-start) | copy-done | bytes 1228824
  1.9 1.5 %convolution_convert_fusion.1 = bf16[192,960]{1,0:T(8,128)(2,1)S(1)} fusion(bf16[192,640]{1,0:T(8,128)(2,1)} %bitcast.89, bf16[640,960]{0,1:T(8,128)(2,1)S(1)} %copy-done), kind=kOutput, calls=%fused_computation.14 | convolution fusion | flops 236113920 | bytes 1843200 | tf_op jit(solution)/shard_map/dot_general | solution.py:187
  3.4 0.8 fusion.39
  4.2 0.3 convolution_convert_fusion.3
  4.5 0.1 pad_maximum_fusion.4
  4.7 5.5 %collective-permute-start.5 = (bf16[6,32,640]{2,1,0:T(8,128)(2,1)S(1)}, bf16[6,32,640]{2,1,0:T(8,128)(2,1)}, u32[]{:S(2)}, u32[]{:S(2)}) collective-permute-start(bf16[6,32,640]{2,1,0:T(8,128)(2,1)S(1)} %bitcast.73), channel_id=1, source_target_pairs={{2,0},{4,2},{6,4},{8,6},{10,8},{12,10},{14,12},{16,14},{18,16},{20... | collective-permute-start | bytes 737288 | tf_op jit(solution)/shard_map/ppermute | solution.py:153
  10.2 0.1 copy.28
  10.3 0.1 reshape.299
  10.5 0.2 copy.30
  10.8 0.8 sub.133
  11.8 4.4 %collective-permute-start.9 = (f32[6,32,10]{1,0,2:T(8,128)S(1)}, f32[6,32,10]{1,0,2:T(8,128)S(1)}, u32[]{:S(2)}, u32[]{:S(2)}) collective-permute-start(f32[6,32,10]{1,0,2:T(8,128)S(1)} %reshape.291), channel_id=1, source_target_pairs={{2,0},{4,2},{6,4},{8,6},{10,8},{12,10},{14,12},{16,14},{18,16},{20... | collective-permute-start | bytes 23048 | tf_op jit(solution)/shard_map/ppermute | solution.py:153
  16.2 0.1 slice.75
  16.4 4.5 %collective-permute-start.1 = (bf16[6,32,640]{2,1,0:T(8,128)(2,1)S(1)}, bf16[6,32,640]{2,1,0:T(8,128)(2,1)S(1)}, u32[]{:S(2)}, u32[]{:S(2)}) collective-permute-start(bf16[6,32,640]{2,1,0:T(8,128)(2,1)S(1)} %bitcast.77), channel_id=1, source_target_pairs={{2,0},{4,2},{6,4},{8,6},{10,8},{12,10},{14,12},{16,14},{18,16},{20... | collective-permute-start | bytes 737288 | tf_op jit(solution)/shard_map/ppermute | solution.py:153
  20.9 2.0 %fusion.7 = bf16[640,320]{0,1:T(8,128)(2,1)} fusion(bf16[6,32,640]{2,1,0:T(8,128)(2,1)S(1)} %copy-done.6, bf16[6,32,320]{2,1,0:T(8,128)(2,1)} %param.9), kind=kOutput, calls=%fused_computation.13 | convolution fusion | flops 78848000 | bytes 778240 | tf_op jit(solution)/shard_map/dot_general | solution.py:193
  22.9 1.1 fusion.18
  24.0 0.1 fusion.40
  24.1 1.6 %collective-permute-start.11 = (f32[18,6,10]{1,0,2:T(8,128)S(1)}, f32[18,6,10]{1,0,2:T(8,128)S(1)}, u32[]{:S(2)}, u32[]{:S(2)}) collective-permute-start(f32[18,6,10]{1,0,2:T(8,128)S(1)} %get-tuple-element.21), channel_id=1, source_target_pairs={{1,0},{0,1},{3,2},{2,3},{5,4},{4,5},{7,6},{6,7},{9,8},{8,9},{11,10... | collective-permute-start | bytes 12968 | tf_op jit(solution)/shard_map/ppermute | solution.py:153
  25.7 0.5 collective-permute-start.10
  26.2 1.1 fusion.16
  27.3 0.1 copy.27
  27.4 0.8 copy.32
  28.2 0.8 copy.34
  29.1 2.8 %collective-permute-done.10 = f32[18,6,10]{1,0,2:T(8,128)S(1)} collective-permute-done((f32[18,6,10]{1,0,2:T(8,128)S(1)}, f32[18,6,10]{1,0,2:T(8,128)S(1)}, u32[]{:S(2)}, u32[]{:S(2)}) %collective-permute-start.10) | collective-permute-done | bytes 4352 | tf_op jit(solution)/shard_map/ppermute | solution.py:150
  31.9 0.2 pad_maximum_fusion.14
  32.0 0.1 reshape.292
  32.2 1.0 pad_maximum_fusion.9
  33.1 1.2 %collective-permute-start.7 = (bf16[18,6,640]{2,1,0:T(8,128)(2,1)S(1)}, bf16[18,6,640]{2,1,0:T(8,128)(2,1)S(1)}, u32[]{:S(2)}, u32[]{:S(2)}) collective-permute-start(bf16[18,6,640]{2,1,0:T(8,128)(2,1)S(1)} %get-tuple-element.16), channel_id=1, source_target_pairs={{1,0},{0,1},{3,2},{2,3},{5,4},{4,5},{7,6},{6,7},{9,8},{8,9},{11,10... | collective-permute-start | bytes 414728 | tf_op jit(solution)/shard_map/ppermute | solution.py:153
  34.4 0.9 collective-permute-start.6
  35.2 0.6 fusion.41
  35.9 1.5 %collective-permute-done = bf16[6,32,640]{2,1,0:T(8,128)(2,1)S(1)} collective-permute-done((bf16[6,32,640]{2,1,0:T(8,128)(2,1)S(1)}, bf16[6,32,640]{2,1,0:T(8,128)(2,1)S(1)}, u32[]{:S(2)}, u32[]{:S(2)}) %collective-permute-start) | collective-permute-done | bytes 245792 | tf_op jit(solution)/shard_map/ppermute | solution.py:150
  37.4 0.8 pad_maximum_fusion.12
  38.2 1.5 %collective-permute-start.3 = (bf16[18,6,640]{2,1,0:T(8,128)(2,1)}, bf16[18,6,640]{2,1,0:T(8,128)(2,1)}, u32[]{:S(2)}, u32[]{:S(2)}) collective-permute-start(bf16[18,6,640]{2,1,0:T(8,128)(2,1)} %get-tuple-element.14), channel_id=1, source_target_pairs={{1,0},{0,1},{3,2},{2,3},{5,4},{4,5},{7,6},{6,7},{9,8},{8,9},{11,10... | collective-permute-start | bytes 414728 | tf_op jit(solution)/shard_map/ppermute | solution.py:153
  39.7 0.5 collective-permute-start.2
  40.3 0.2 collective-permute-done.7
  40.4 2.0 %collective-permute-done.6 = bf16[18,6,640]{2,1,0:T(8,128)(2,1)S(1)} collective-permute-done((bf16[18,6,640]{2,1,0:T(8,128)(2,1)S(1)}, bf16[18,6,640]{2,1,0:T(8,128)(2,1)S(1)}, u32[]{:S(2)}, u32[]{:S(2)}) %collective-permute-start.6) | collective-permute-done | bytes 138272 | tf_op jit(solution)/shard_map/ppermute | solution.py:150
  42.4 1.5 %pad_maximum_fusion.2 = bf16[18,44,640]{2,1,0:T(8,128)(2,1)S(1)} fusion(bf16[18,6,640]{2,1,0:T(8,128)(2,1)S(1)} %collective-permute-done.7, bf16[6,32,640]{2,1,0:T(8,128)(2,1)} %collective-permute-done.5, bf16[6,32,640]{2,1,0:T(8,128)(2,1)S(1)} %bitcast.76, bf16[6,32,640]{2,1,0:T(8,128)(2,1)} %collective-permute-done.4, ...), kind=kLoop, calls=%fused_computation.23 | loop fusion | flops 5068800 | bytes 2027520 | tf_op jit(solution)/shard_map/concatenate | solution.py:154
  43.9 0.2 reshape.288
  44.1 1.1 fusion.38
  45.2 2.2 %copy.41 = bf16[792,320]{0,1:T(8,128)(2,1)} copy(bf16[792,320]{1,0:T(8,128)(2,1)} %get-tuple-element.12) | data formatting | bytes 1013760
  47.4 1.1 copy.40
  48.5 1.5 %pad_maximum_fusion.1 = bf16[18,44,640]{2,1,0:T(8,128)(2,1)S(1)} fusion(bf16[18,6,640]{2,1,0:T(8,128)(2,1)} %collective-permute-done.3, bf16[6,32,640]{2,1,0:T(8,128)(2,1)S(1)} %copy-done.8, bf16[6,32,640]{2,1,0:T(8,128)(2,1)S(1)} %bitcast.80, bf16[6,32,640]{2,1,0:T(8,128)(2,1)S(1)} %copy-done.10, bf16[18,6,640]{2,1,0:T(8,128)(2,1)} %collective-permute-done.2), kind=kLoop, calls=%fused_computation.22 | loop fusion | flops 5068800 | bytes 2027520 | tf_op jit(solution)/shard_map/concatenate | solution.py:154
  50.0 0.2 reshape.280
  50.2 1.1 fusion.37
  51.3 1.4 %copy.26 = bf16[792,320]{0,1:T(8,128)(2,1)S(1)} copy(bf16[792,320]{1,0:T(8,128)(2,1)} %get-tuple-element.10) | data formatting | bytes 1013760 | tf_op jit(solution)/shard_map/slice | solution.py:220
  52.7 1.1 copy.29
  53.8 0.7 fusion.43
  54.5 0.4 copy-done.17
  54.9 1.6 %fusion.12 = bf16[5,64,192]{2,1,0:T(8,128)(2,1)} fusion(bf16[792,5,64]{0,2,1:T(8,128)(2,1)S(1)} %bitcast.86, f32[5,792,192]{1,2,0:T(8,128)S(1)} %fusion.43, f32[5,792]{1,0:T(8,128)S(1)} %copy-done.25, pred[792,192]{0,1:T(8,128)(4,1)S(1)} %copy-done.21), kind=kOutput, calls=%fused_computation.20 | convolution fusion | flops 100423680 | bytes 3838944 | tf_op jit(solution)/shard_map/het,ehd->thd/dot_general | solution.py:258
  56.5 4.3 %fusion.11 = bf16[5,64,192]{2,1,0:T(8,128)(2,1)} fusion(bf16[792,5,64]{0,2,1:T(8,128)(2,1)S(1)} %bitcast.70, f32[5,792,192]{1,2,0:T(8,128)} %copy-done.1, bf16[792,5,64]{0,2,1:T(8,128)(2,1)S(1)} %bitcast.87, bf16[192,5,64]{0,2,1:T(8,128)(2,1)S(1)} %bitcast.92, f32[5,792]{1,0:T(8,128)S(1)} %copy-done.24, f32[5,792]{1,0:T(8,128)S(1)} %copy-done.25, ...), kind=kOutput, calls=%fused_computation.19 | convolution fusion | flops 199326720 | bytes 4484544 | tf_op jit(solution)/shard_map/het,ehd->thd/dot_general | solution.py:253
  60.8 2.4 %fusion.42 = f32[5,192,792]{2,1,0:T(8,128)} fusion(bf16[192,5,64]{0,2,1:T(8,128)(2,1)S(1)} %bitcast.82, bf16[792,5,64]{0,2,1:T(8,128)(2,1)S(1)} %bitcast.71), kind=kOutput, calls=%fused_computation.80 | convolution fusion | flops 97320960 | bytes 3671040 | tf_op jit(solution)/shard_map/thd,ehd->hte/dot_general | solution.py:223
  63.2 3.8 %fusion.10 = bf16[5,64,192]{2,1,0:T(8,128)(2,1)S(1)} fusion(bf16[792,5,64]{0,2,1:T(8,128)(2,1)S(1)} %bitcast.72, f32[5,192,792]{2,1,0:T(8,128)} %fusion.42, bf16[192,5,64]{0,2,1:T(8,128)(2,1)S(1)} %bitcast.85, bf16[792,5,64]{0,2,1:T(8,128)(2,1)S(1)} %bitcast.88, f32[5,192]{1,0:T(8,128)S(1)} %bitcast.94, f32[5,192]{1,0:T(8,128)S(1)} %sub.133, ...), kind=kOutput, calls=%fused_computation.18 | convolution fusion | flops 199326720 | bytes 4460544 | tf_op jit(solution)/shard_map/hte,ehd->thd/dot_general | solution.py:232
  67.0 1.2 %convolution_convert_fusion.2 = bf16[192,640]{1,0:T(8,128)(2,1)} fusion(bf16[640,960]{0,1:T(8,128)(2,1)S(1)} %copy-done, bf16[192,320]{0,1:T(8,128)(2,1)S(1)} %bitcast.96, bf16[192,320]{0,1:T(8,128)(2,1)S(1)} %bitcast.98, bf16[192,320]{0,1:T(8,128)(2,1)S(1)} %bitcast.100), kind=kOutput, calls=%fused_computation.15 | convolution fusion | flops 237158400 | bytes 1843200 | tf_op jit(solution)/shard_map/dot_general | solution.py:271
  68.3 0.5 fusion.4
  68.8 0.1 pad_maximum_fusion
  69.0 2.5 %copy.35 = bf16[640,1280]{1,0:T(8,128)(2,1)} copy(bf16[640,1280]{0,1:T(8,128)(2,1)S(1)} %pad_maximum_fusion) | data formatting | bytes 3276800 | tf_op jit(solution)/shard_map/concatenate | solution.py:278
  71.4 3.5 %convert_element_type.42 = bf16[4,4,40,2,640]{4,3,2,1,0:T(2,128)(2,1)S(1)} reshape(bf16[640,1280]{1,0:T(8,128)(2,1)} %copy.35) | data formatting | bytes 3276800 | tf_op jit(solution)/shard_map/convert_element_type | solution.py:117
  74.9 1.4 %copy.44 = bf16[4,4,40,2,640]{4,2,1,0,3:T(8,128)(2,1)} copy(bf16[4,4,40,2,640]{4,3,2,1,0:T(2,128)(2,1)S(1)} %convert_element_type.42) | data formatting | bytes 3276800 | tf_op jit(solution)/shard_map/convert_element_type | solution.py:117
  76.3 35.2 %weight_sums.1 = bf16[2,4,4,40,640]{4,3,2,1,0:T(8,128)(2,1)} custom-call(bf16[2,4,4,40,640]{4,3,2,1,0:T(8,128)(2,1)} %bitcast.66), custom_call_target="tpu_custom_call" | custom-call | tf_op jit(solution)/shard_map/weight_sums/pallas_call | solution.py:120
  111.5 3.1 %copy.37 = bf16[4,4,40,2,640]{4,3,2,1,0:T(2,128)(2,1)S(1)} copy(bf16[4,4,40,2,640]{4,2,1,0,3:T(8,128)(2,1)} %bitcast.67) | data formatting | bytes 3276800 | tf_op jit(solution)/shard_map/transpose | solution.py:141
  114.7 0.3 copy.42
  114.9 0.2 slice.87
  115.1 0.2 slice_bitcast_fusion
  115.3 1.4 %copy.38 = bf16[640,960]{0,1:T(8,128)(2,1)} copy(bf16[640,960]{1,0:T(8,128)(2,1)S(1)} %slice.87) | data formatting | bytes 2457600
  116.8 1.0 copy.39
  (72 shorter events, 0.4 us)
Async XLA Ops:
  0.6 1.3 %copy-start = (bf16[640,960]{0,1:T(8,128)(2,1)S(1)}, bf16[640,960]{0,1:T(8,128)(2,1)}, u32[]{:S(2)}) copy-start(bf16[640,960]{0,1:T(8,128)(2,1)} %param.7) | copy-start | bytes 3686404
  0.6 3.6 %copy-start.6 = (bf16[6,32,640]{2,1,0:T(8,128)(2,1)S(1)}, bf16[6,32,640]{2,1,0:T(8,128)(2,1)}, u32[]{:S(2)}) copy-start(bf16[6,32,640]{2,1,0:T(8,128)(2,1)} %param.11) | copy-start | bytes 737284
  0.7 3.6 %copy-start.19 = (bf16[320,640]{1,0:T(8,128)(2,1)S(1)}, bf16[320,640]{1,0:T(8,128)(2,1)}, u32[]{:S(2)}) copy-start(bf16[320,640]{1,0:T(8,128)(2,1)} %param.8) | copy-start | bytes 1228804
  0.7 9.7 %copy-start.16 = (bf16[6,32,320]{2,1,0:T(8,128)(2,1)S(1)}, bf16[6,32,320]{2,1,0:T(8,128)(2,1)}, u32[]{:S(2)}) copy-start(bf16[6,32,320]{2,1,0:T(8,128)(2,1)} %param.9) | copy-start | bytes 368644
  4.7 27.5 %collective-permute-start.5 = (bf16[6,32,640]{2,1,0:T(8,128)(2,1)S(1)}, bf16[6,32,640]{2,1,0:T(8,128)(2,1)}, u32[]{:S(2)}, u32[]{:S(2)}) collective-permute-start(bf16[6,32,640]{2,1,0:T(8,128)(2,1)S(1)} %bitcast.73), channel_id=1, source_target_pairs={{2,0},{4,2},{6,4},{8,6},{10,8},{12,10},{14,12},{16,14},{18,16},{20... | collective-permute-start | bytes 737288 | tf_op jit(solution)/shard_map/ppermute | solution.py:153
  10.2 22.0 %collective-permute-start.4 = (bf16[6,32,640]{2,1,0:T(8,128)(2,1)S(1)}, bf16[6,32,640]{2,1,0:T(8,128)(2,1)}, u32[]{:S(2)}, u32[]{:S(2)}) collective-permute-start(bf16[6,32,640]{2,1,0:T(8,128)(2,1)S(1)} %bitcast.74), channel_id=1, source_target_pairs={{0,2},{2,4},{4,6},{6,8},{8,10},{10,12},{12,14},{14,16},{16,18},{18... | collective-permute-start | bytes 737288 | tf_op jit(solution)/shard_map/ppermute | solution.py:150
  10.3 13.7 %copy-start.12 = (bf16[192,320]{0,1:T(8,128)(2,1)}, bf16[192,320]{0,1:T(8,128)(2,1)S(1)}, u32[]{:S(2)}) copy-start(bf16[192,320]{0,1:T(8,128)(2,1)S(1)} %copy.28) | copy-start | bytes 368644
  10.8 16.7 %copy-start.15 = (bf16[192,320]{1,0:T(8,128)(2,1)S(1)}, bf16[192,320]{1,0:T(8,128)(2,1)}, u32[]{:S(2)}) copy-start(bf16[192,320]{1,0:T(8,128)(2,1)} %get-tuple-element.18) | copy-start | bytes 368644
  10.8 17.4 %copy-start.14 = (bf16[192,320]{1,0:T(8,128)(2,1)S(1)}, bf16[192,320]{1,0:T(8,128)(2,1)}, u32[]{:S(2)}) copy-start(bf16[192,320]{1,0:T(8,128)(2,1)} %get-tuple-element.17) | copy-start | bytes 368644
  11.8 12.2 %collective-permute-start.9 = (f32[6,32,10]{1,0,2:T(8,128)S(1)}, f32[6,32,10]{1,0,2:T(8,128)S(1)}, u32[]{:S(2)}, u32[]{:S(2)}) collective-permute-start(f32[6,32,10]{1,0,2:T(8,128)S(1)} %reshape.291), channel_id=1, source_target_pairs={{2,0},{4,2},{6,4},{8,6},{10,8},{12,10},{14,12},{16,14},{18,16},{20... | collective-permute-start | bytes 23048 | tf_op jit(solution)/shard_map/ppermute | solution.py:153
  16.2 7.8 %collective-permute-start.8 = (f32[6,32,10]{1,0,2:T(8,128)S(1)}, f32[6,32,10]{1,0,2:T(8,128)S(1)}, u32[]{:S(2)}, u32[]{:S(2)}) collective-permute-start(f32[6,32,10]{1,0,2:T(8,128)S(1)} %reshape.291), channel_id=1, source_target_pairs={{0,2},{2,4},{4,6},{6,8},{8,10},{10,12},{12,14},{14,16},{16,18},{18... | collective-permute-start | bytes 23048 | tf_op jit(solution)/shard_map/ppermute | solution.py:150
  16.4 21.0 %copy-start.3 = (bf16[192,640]{1,0:T(8,128)(2,1)}, bf16[192,640]{1,0:T(8,128)(2,1)S(1)}, u32[]{:S(2)}) copy-start(bf16[192,640]{1,0:T(8,128)(2,1)S(1)} %slice.75) | copy-start | bytes 737284
  16.4 19.5 %collective-permute-start.1 = (bf16[6,32,640]{2,1,0:T(8,128)(2,1)S(1)}, bf16[6,32,640]{2,1,0:T(8,128)(2,1)S(1)}, u32[]{:S(2)}, u32[]{:S(2)}) collective-permute-start(bf16[6,32,640]{2,1,0:T(8,128)(2,1)S(1)} %bitcast.77), channel_id=1, source_target_pairs={{2,0},{4,2},{6,4},{8,6},{10,8},{12,10},{14,12},{16,14},{18,16},{20... | collective-permute-start | bytes 737288 | tf_op jit(solution)/shard_map/ppermute | solution.py:153
  24.1 4.9 %collective-permute-start.11 = (f32[18,6,10]{1,0,2:T(8,128)S(1)}, f32[18,6,10]{1,0,2:T(8,128)S(1)}, u32[]{:S(2)}, u32[]{:S(2)}) collective-permute-start(f32[18,6,10]{1,0,2:T(8,128)S(1)} %get-tuple-element.21), channel_id=1, source_target_pairs={{1,0},{0,1},{3,2},{2,3},{5,4},{4,5},{7,6},{6,7},{9,8},{8,9},{11,10... | collective-permute-start | bytes 12968 | tf_op jit(solution)/shard_map/ppermute | solution.py:153
  25.7 6.2 %collective-permute-start.10 = (f32[18,6,10]{1,0,2:T(8,128)S(1)}, f32[18,6,10]{1,0,2:T(8,128)S(1)}, u32[]{:S(2)}, u32[]{:S(2)}) collective-permute-start(f32[18,6,10]{1,0,2:T(8,128)S(1)} %get-tuple-element.20), channel_id=1, source_target_pairs={{0,1},{1,0},{2,3},{3,2},{4,5},{5,4},{6,7},{7,6},{8,9},{9,8},{10,11... | collective-permute-start | bytes 12968 | tf_op jit(solution)/shard_map/ppermute | solution.py:150
  29.1 8.3 %collective-permute-start = (bf16[6,32,640]{2,1,0:T(8,128)(2,1)S(1)}, bf16[6,32,640]{2,1,0:T(8,128)(2,1)S(1)}, u32[]{:S(2)}, u32[]{:S(2)}) collective-permute-start(bf16[6,32,640]{2,1,0:T(8,128)(2,1)S(1)} %bitcast.78), channel_id=1, source_target_pairs={{0,2},{2,4},{4,6},{6,8},{8,10},{10,12},{12,14},{14,16},{16,18},{18... | collective-permute-start | bytes 737288 | tf_op jit(solution)/shard_map/ppermute | solution.py:150
  33.1 7.3 %collective-permute-start.7 = (bf16[18,6,640]{2,1,0:T(8,128)(2,1)S(1)}, bf16[18,6,640]{2,1,0:T(8,128)(2,1)S(1)}, u32[]{:S(2)}, u32[]{:S(2)}) collective-permute-start(bf16[18,6,640]{2,1,0:T(8,128)(2,1)S(1)} %get-tuple-element.16), channel_id=1, source_target_pairs={{1,0},{0,1},{3,2},{2,3},{5,4},{4,5},{7,6},{6,7},{9,8},{8,9},{11,10... | collective-permute-start | bytes 414728 | tf_op jit(solution)/shard_map/ppermute | solution.py:153
  34.4 8.0 %collective-permute-start.6 = (bf16[18,6,640]{2,1,0:T(8,128)(2,1)S(1)}, bf16[18,6,640]{2,1,0:T(8,128)(2,1)S(1)}, u32[]{:S(2)}, u32[]{:S(2)}) collective-permute-start(bf16[18,6,640]{2,1,0:T(8,128)(2,1)S(1)} %get-tuple-element.15), channel_id=1, source_target_pairs={{0,1},{1,0},{2,3},{3,2},{4,5},{5,4},{6,7},{7,6},{8,9},{9,8},{10,11... | collective-permute-start | bytes 414728 | tf_op jit(solution)/shard_map/ppermute | solution.py:150
  35.8 6.5 %copy-start.7 = (bf16[6,32,640]{2,1,0:T(8,128)(2,1)}, bf16[6,32,640]{2,1,0:T(8,128)(2,1)S(1)}, u32[]{:S(2)}) copy-start(bf16[6,32,640]{2,1,0:T(8,128)(2,1)S(1)} %collective-permute-done.1) | copy-start | bytes 737284
  37.4 3.0 %copy-start.9 = (bf16[6,32,640]{2,1,0:T(8,128)(2,1)}, bf16[6,32,640]{2,1,0:T(8,128)(2,1)S(1)}, u32[]{:S(2)}) copy-start(bf16[6,32,640]{2,1,0:T(8,128)(2,1)S(1)} %collective-permute-done) | copy-start | bytes 737284
  38.2 10.3 %collective-permute-start.3 = (bf16[18,6,640]{2,1,0:T(8,128)(2,1)}, bf16[18,6,640]{2,1,0:T(8,128)(2,1)}, u32[]{:S(2)}, u32[]{:S(2)}) collective-permute-start(bf16[18,6,640]{2,1,0:T(8,128)(2,1)} %get-tuple-element.14), channel_id=1, source_target_pairs={{1,0},{0,1},{3,2},{2,3},{5,4},{4,5},{7,6},{6,7},{9,8},{8,9},{11,10... | collective-permute-start | bytes 414728 | tf_op jit(solution)/shard_map/ppermute | solution.py:153
  39.7 8.8 %collective-permute-start.2 = (bf16[18,6,640]{2,1,0:T(8,128)(2,1)}, bf16[18,6,640]{2,1,0:T(8,128)(2,1)}, u32[]{:S(2)}, u32[]{:S(2)}) collective-permute-start(bf16[18,6,640]{2,1,0:T(8,128)(2,1)} %get-tuple-element.13), channel_id=1, source_target_pairs={{0,1},{1,0},{2,3},{3,2},{4,5},{5,4},{6,7},{7,6},{8,9},{9,8},{10,11... | collective-permute-start | bytes 414728 | tf_op jit(solution)/shard_map/ppermute | solution.py:150
  45.2 3.3 %copy-start.4 = (bf16[192,640]{1,0:T(8,128)(2,1)S(1)}, bf16[192,640]{1,0:T(8,128)(2,1)}, u32[]{:S(2)}) copy-start(bf16[192,640]{1,0:T(8,128)(2,1)} %copy-done.3) | copy-start | bytes 737284
  45.2 3.3 %copy-start.8 = (bf16[6,32,640]{2,1,0:T(8,128)(2,1)S(1)}, bf16[6,32,640]{2,1,0:T(8,128)(2,1)}, u32[]{:S(2)}) copy-start(bf16[6,32,640]{2,1,0:T(8,128)(2,1)} %copy-done.7) | copy-start | bytes 737284
  45.2 3.3 %copy-start.10 = (bf16[6,32,640]{2,1,0:T(8,128)(2,1)S(1)}, bf16[6,32,640]{2,1,0:T(8,128)(2,1)}, u32[]{:S(2)}) copy-start(bf16[6,32,640]{2,1,0:T(8,128)(2,1)} %copy-done.9) | copy-start | bytes 737284
  51.3 2.5 %copy-start.2 = (bf16[792,320]{0,1:T(8,128)(2,1)S(1)}, bf16[792,320]{0,1:T(8,128)(2,1)}, u32[]{:S(2)}) copy-start(bf16[792,320]{0,1:T(8,128)(2,1)} %copy.40) | copy-start | bytes 1520644
  51.3 2.5 %copy-start.11 = (bf16[192,320]{0,1:T(8,128)(2,1)S(1)}, bf16[192,320]{0,1:T(8,128)(2,1)}, u32[]{:S(2)}) copy-start(bf16[192,320]{0,1:T(8,128)(2,1)} %copy.32) | copy-start | bytes 368644
  53.8 1.1 copy-start.17
  53.8 1.1 copy-start.21
  53.8 1.1 copy-start.25
  54.5 2.0 %copy-start.1 = (f32[5,792,192]{1,2,0:T(8,128)}, f32[5,792,192]{1,2,0:T(8,128)S(1)}, u32[]{:S(2)}) copy-start(f32[5,792,192]{1,2,0:T(8,128)S(1)} %fusion.43) | copy-start | bytes 9123844
  54.9 1.6 %copy-start.23 = (bf16[192,320]{0,1:T(8,128)(2,1)S(1)}, bf16[192,320]{0,1:T(8,128)(2,1)}, u32[]{:S(2)}) copy-start(bf16[192,320]{0,1:T(8,128)(2,1)} %copy.34) | copy-start | bytes 368644
  54.9 1.6 %copy-start.24 = (f32[5,792]{1,0:T(8,128)S(1)}, f32[5,792]{1,0:T(8,128)}, u32[]{:S(2)}) copy-start(f32[5,792]{1,0:T(8,128)} %get-tuple-element.22) | copy-start | bytes 47524
  60.8 2.4 %copy-start.13 = (bf16[192,320]{0,1:T(8,128)(2,1)S(1)}, bf16[192,320]{0,1:T(8,128)(2,1)}, u32[]{:S(2)}) copy-start(bf16[192,320]{0,1:T(8,128)(2,1)} %copy-done.12) | copy-start | bytes 368644
  60.8 2.4 %copy-start.18 = (bf16[792,320]{0,1:T(8,128)(2,1)S(1)}, bf16[792,320]{0,1:T(8,128)(2,1)}, u32[]{:S(2)}) copy-start(bf16[792,320]{0,1:T(8,128)(2,1)} %copy.29) | copy-start | bytes 1520644
  60.8 2.4 %copy-start.22 = (pred[192,792]{1,0:T(8,128)(4,1)S(1)}, pred[192,792]{1,0:T(8,128)(4,1)}, u32[]{:S(2)}) copy-start(pred[192,792]{1,0:T(8,128)(4,1)} %fusion.16) | copy-start | bytes 456196
  63.2 3.8 %copy-start.26 = (bf16[5,64,192]{2,1,0:T(8,128)(2,1)S(1)}, bf16[5,64,192]{2,1,0:T(8,128)(2,1)}, u32[]{:S(2)}) copy-start(bf16[5,64,192]{2,1,0:T(8,128)(2,1)} %fusion.12) | copy-start | bytes 368644
  63.2 3.8 %copy-start.27 = (bf16[5,64,192]{2,1,0:T(8,128)(2,1)S(1)}, bf16[5,64,192]{2,1,0:T(8,128)(2,1)}, u32[]{:S(2)}) copy-start(bf16[5,64,192]{2,1,0:T(8,128)(2,1)} %fusion.11) | copy-start | bytes 368644
  67.0 1.2 %copy-start.20 = (bf16[6,32,640]{2,1,0:T(8,128)(2,1)S(1)}, bf16[6,32,640]{2,1,0:T(8,128)(2,1)}, u32[]{:S(2)}) copy-start(bf16[6,32,640]{2,1,0:T(8,128)(2,1)} %param.6) | copy-start | bytes 737284
  67.0 1.8 %copy-start.5 = (bf16[640,320]{0,1:T(8,128)(2,1)S(1)}, bf16[640,320]{0,1:T(8,128)(2,1)}, u32[]{:S(2)}) copy-start(bf16[640,320]{0,1:T(8,128)(2,1)} %fusion.7) | copy-start | bytes 1228804

commit v2 on v1

--- a/solution.py
+++ b/solution.py
@@ -2,6 +2,7 @@
 
 import jax
 import jax.numpy as jnp
+import numpy as np
 from jax import lax
 from jax.experimental import pallas as pl
 from jax.experimental.pallas import tpu as pltpu
@@ -24,6 +25,9 @@
     core, lane, z = row % 2, (row // 2) % 2, row // 4
     p = lane * width + col
     partner = (row + 1 - 2 * core, col)
+    half = x_ref.shape[3] // 2
+    lanes = pl.ds(pl.multiple_of(core * half, 128), half)
+    others = pl.ds(pl.multiple_of((1 - core) * half, 128), half)
 
     def plane_peer(k):
         q = (p + k) % planes
@@ -53,12 +57,12 @@
     pair, started = {}, []
     for k in order:
         q = (p + k) % planes
-        pair[k] = send(x_ref.at[1 - core, q], recv1.at[k], s1.at[k], r1.at[k], partner)
+        pair[k] = send(x_ref.at[q, :, :, others], recv1.at[k], s1.at[k], r1.at[k], partner)
     across = {}
     for k in order:
         q, device = plane_peer(k)
         pair[k].wait_recv()
-        total = x_ref[core, q].astype(jnp.float32) + recv1[k].astype(jnp.float32)
+        total = x_ref[q, :, :, lanes].astype(jnp.float32) + recv1[k].astype(jnp.float32)
         sum1[k] = total.astype(jnp.bfloat16)
         if k:
             across[k] = send(sum1.at[k], recv2.at[k - 1], s2.at[k - 1], r2.at[k - 1], device)
@@ -75,9 +79,9 @@
     for k in range(1, depth):
         deep[k].wait_recv()
         total = total + recv3[k - 1].astype(jnp.float32)
-    o_ref[core, p, z] = (total * factor).astype(jnp.bfloat16)
-
-    own = o_ref.at[core, p, z]
+    o_ref[p, z, :, lanes] = (total * factor).astype(jnp.bfloat16)
+
+    own = o_ref.at[p, z, :, lanes]
     zcopies, pcopies = {}, {}
     for k in range(1, depth):
         zcopies[k] = send(own, own, zs.at[k - 1], zr.at[k - 1], z_peer(k)[1])
@@ -92,11 +96,11 @@
     share(0, own)
     for k in range(1, depth):
         zcopies[k].wait_recv()
-        share(k, o_ref.at[core, p, (z - k + depth) % depth])
+        share(k, o_ref.at[p, (z - k + depth) % depth, :, lanes])
     for kz in range(depth):
         for k in range(1, planes):
             pcopies[k, kz].wait_recv()
-            piece = o_ref.at[core, (p - k + planes) % planes, (z - kz + depth) % depth]
+            piece = o_ref.at[(p - k + planes) % planes, (z - kz + depth) % depth, :, lanes]
             started.append(send(piece, piece, cs.at[k, kz], cr.at[k, kz], partner))
     for copy in started:
         copy.wait_recv()
@@ -112,14 +116,14 @@
     planes, depth = 2 * width, max(count // 4, 1)
     half = columns // 2
     if count % 4 or rows % (planes * depth * 8) or columns % 256 or depth < 2:
-        return (lax.psum(parts, ("rows", "cols")) * factor).astype(jnp.bfloat16)
+        return (lax.psum(parts.astype(jnp.float32), ("rows", "cols")) * factor).astype(jnp.bfloat16)
     high = rows // (planes * depth)
-    x = parts.astype(jnp.bfloat16).reshape(planes, depth, high, 2, half).transpose(3, 0, 1, 2, 4)
+    x = parts.astype(jnp.bfloat16).reshape(planes, depth, high, columns)
     low = jnp.bfloat16
     dma = pltpu.SemaphoreType.DMA
     out = pl.pallas_call(
         functools.partial(reduce_kernel, planes, depth, width, factor),
-        out_shape=jax.ShapeDtypeStruct((2, planes, depth, high, half), low),
+        out_shape=jax.ShapeDtypeStruct((planes, depth, high, columns), low),
         in_specs=[pl.BlockSpec(memory_space=pltpu.VMEM)],
         out_specs=pl.BlockSpec(memory_space=pltpu.VMEM),
         scratch_shapes=[
@@ -138,7 +142,7 @@
         compiler_params=pltpu.CompilerParams(collective_id=0, has_side_effects=True),
         name="weight_sums",
     )(x)
-    return out.transpose(1, 2, 3, 0, 4).reshape(rows, columns)
+    return out.reshape(rows, columns)
 
 
 def padded(block, sides, width):
@@ -280,6 +284,218 @@
     return grad_input, sums[:, :columns], sums[:, columns:].T
 
 
+STATS = 128
+NT = (((1,), (1,)), ((), ()))
+NN = (((1,), (0,)), ((), ()))
+TN = (((0,), (0,)), ((), ()))
+
+
+def dot(a, b, dims=NN):
+    return lax.dot_general(a, b, dims, preferred_element_type=jnp.float32)
+
+
+def terms(x):
+    high = x.astype(jnp.bfloat16).astype(jnp.float32)
+    return high, (x - high).astype(jnp.bfloat16).astype(jnp.float32)
+
+
+def project_kernel(in_ref, wqkv_ref, cot_ref, wout_ref, att_ref, norm_ref, perm_ref, o_ref):
+    tokens, inner = att_ref.shape
+    low = jnp.bfloat16
+    perm = perm_ref[...]
+    projected = dot(in_ref[...], wqkv_ref[...]).astype(low)
+    upstream = dot(cot_ref[...], wout_ref[...], NT).astype(low)
+    width = 3 * inner
+    product = upstream.astype(jnp.float32) * att_ref[...].astype(jnp.float32)
+    lane = lax.broadcasted_iota(jnp.int32, (tokens, STATS), 1)
+    stats = jnp.zeros((tokens, STATS), jnp.float32)
+    norm = norm_ref[...]
+    norm_high, norm_low = terms(norm)
+    norm_high, norm_low = dot(perm, norm_high.astype(low), NT), dot(perm, norm_low.astype(low), NT)
+    for h in range(HEADS):
+        delta = jnp.sum(product[:, h * HEAD_DIM:(h + 1) * HEAD_DIM], axis=1, keepdims=True)
+        high, rest = terms(delta)
+        stats = jnp.where(lane == 2 * HEADS + h, high, stats)
+        stats = jnp.where(lane == 3 * HEADS + h, rest, stats)
+    moved = dot(perm, stats.astype(low))
+    for h in range(HEADS):
+        moved = jnp.where(lane == h, norm_high[:, h:h + 1], moved)
+        moved = jnp.where(lane == HEADS + h, norm_low[:, h:h + 1], moved)
+    rows = jnp.concatenate([projected, upstream], axis=1)
+    o_ref[:, :width + inner] = dot(perm, rows).astype(low)
+    o_ref[:, width + inner:] = moved.astype(low)
+
+
+def halo_kernel(rows_count, edge, x_ref, o_ref, own_sem, rs, rr, xs, xr):
+    row, col = lax.axis_index("rows"), lax.axis_index("cols")
+    tokens = x_ref.shape[0]
+    above = ((row + rows_count - 1) % rows_count, col)
+    below = ((row + 1) % rows_count, col)
+    beside = (row, 1 - col)
+
+    def send(src, dst, ssem, rsem, device):
+        copy = pltpu.make_async_remote_copy(
+            src_ref=src, dst_ref=dst, send_sem=ssem, recv_sem=rsem,
+            device_id=device, device_id_type=MESH,
+        )
+        copy.start()
+        return copy
+
+    barrier = pltpu.get_barrier_semaphore()
+    for peer in (above, below, beside):
+        pl.semaphore_signal(barrier, inc=1, device_id=peer, device_id_type=MESH)
+    pl.semaphore_wait(barrier, 3)
+
+    def band(slot, first, size):
+        return o_ref.at[pl.ds(slot * tokens + first, size), :]
+
+    def side(slot):
+        return o_ref.at[pl.ds(3 * tokens + slot * edge, edge), :]
+
+    rest = tokens - edge
+    head, tail = x_ref.at[pl.ds(0, edge), :], x_ref.at[pl.ds(edge, rest), :]
+    first = {}
+    for slot, device in ((2, above), (0, below)):
+        first[slot] = send(head, band(slot, 0, edge), rs.at[slot, 0], rr.at[slot, 0], device)
+    copies = [send(head, side(1), xs.at[1], xr.at[1], beside)]
+    for slot, device in ((2, above), (0, below)):
+        copies.append(
+            send(tail, band(slot, edge, rest), rs.at[slot, 1], rr.at[slot, 1], device)
+        )
+    own = pltpu.make_async_copy(x_ref, band(1, 0, tokens), own_sem)
+    own.start()
+    for slot in (0, 2):
+        first[slot].wait_recv()
+        copies.append(send(band(slot, 0, edge), side(slot), xs.at[slot], xr.at[slot], beside))
+    for copy in copies:
+        copy.wait_recv()
+    for copy in [*copies, *first.values()]:
+        copy.wait_send()
+    own.wait()
+
+
+def attention_kernel(
+    near_ref, mask_ref, perm_ref, in_ref, cot_ref, att_ref, wqkv_ref, gin_ref, part_ref, grads,
+):
+    tokens, inner = att_ref.shape
+    low = jnp.bfloat16
+    scale = HEAD_DIM ** (-0.5)
+    inside = mask_ref[...] > 0.5
+    own = pl.ds(tokens, tokens)
+    width = 4 * inner
+    near_stats = near_ref[:, width:]
+    own_stats = near_ref[own, width:].astype(jnp.float32)
+    pick_row = lax.broadcasted_iota(jnp.int32, (16, STATS), 0)
+    pick_lane = lax.broadcasted_iota(jnp.int32, (16, STATS), 1)
+    norm_pick = (pick_row < HEADS) & ((pick_lane == pick_row) | (pick_lane == pick_row + HEADS))
+    delta_pick = (pick_row >= HEADS) & (pick_row < 2 * HEADS) & (
+        (pick_lane == pick_row + HEADS) | (pick_lane == pick_row + 2 * HEADS)
+    )
+    pick = jnp.where(norm_pick | delta_pick, 1.0, 0.0).astype(low)
+    near_rows = dot(pick, near_stats, NT)
+    for h in range(HEADS):
+        def part(block, of):
+            return near_ref[of, block * inner + h * HEAD_DIM:block * inner + (h + 1) * HEAD_DIM]
+
+        every = slice(None)
+        query, key, value, up = (part(b, own) for b in range(4))
+        near_query, near_key, near_value, near_up = (part(b, every) for b in range(4))
+        norm = own_stats[:, h:h + 1] + own_stats[:, HEADS + h:HEADS + h + 1]
+        delta = (
+            own_stats[:, 2 * HEADS + h:2 * HEADS + h + 1]
+            + own_stats[:, 3 * HEADS + h:3 * HEADS + h + 1]
+        )
+        scores = dot(query, near_key, NT) * scale
+        weight = jnp.where(inside, jnp.exp(scores - norm), 0.0)
+        score_grad = (weight * (dot(up, near_value, NT) - delta)).astype(low)
+        grad_query = dot(score_grad, near_key) * scale
+        near_norm, near_delta = near_rows[h:h + 1], near_rows[HEADS + h:HEADS + h + 1]
+        scores = dot(key, near_query, NT) * scale
+        weight = jnp.where(inside, jnp.exp(scores - near_norm), 0.0)
+        score_grad = (weight * (dot(value, near_up, NT) - near_delta)).astype(low)
+        grad_key = dot(score_grad, near_query) * scale
+        grad_value = dot(weight.astype(low), near_up)
+        for block, grad in enumerate((grad_query, grad_key, grad_value)):
+            at = block * inner + h * HEAD_DIM
+            grads[:, at:at + HEAD_DIM] = grad.astype(low)
+    grad_proj = dot(perm_ref[...], grads[...], TN).astype(low)
+    gin_ref[...] = dot(grad_proj, wqkv_ref[...], NT).astype(low)
+    part_ref[:, :3 * inner] = dot(in_ref[...], grad_proj, TN).astype(low)
+    part_ref[:, 3 * inner:] = dot(cot_ref[...], att_ref[...], TN).astype(low)
+
+
+def banded(inputs, qkv_weight, out_weight, attn_out, log_norm, cotangent):
+    rows_dev, cols_dev, model_width = inputs.shape
+    tokens = rows_dev * cols_dev
+    inner = HEADS * HEAD_DIM
+    rows_count = lax.axis_size("rows")
+    grid_rows = rows_count * rows_dev
+    edge = -(-2 * RADIUS * rows_dev // 16) * 16
+    near = 3 * (tokens + edge)
+    low = jnp.bfloat16
+    flat_in = inputs.reshape(tokens, model_width)
+    flat_cot = cotangent.reshape(tokens, model_width)
+    flat_att = attn_out.reshape(tokens, inner)
+    cells = [(r, c) for r in range(rows_dev) for c in range(cols_dev)]
+    outer = [(r, c) for r, c in cells if c < RADIUS or c >= cols_dev - RADIUS]
+    order = outer + [(r, c) for r, c in cells if RADIUS <= c < cols_dev - RADIUS]
+    own_row = np.array([r for r, c in order])
+    own_col = np.array([c for r, c in order])
+    perm = np.zeros((tokens, tokens), np.float32)
+    perm[np.arange(tokens), own_row * cols_dev + own_col] = 1.0
+    shifts = [-rows_dev, 0, rows_dev]
+    beside = np.where(own_col < cols_dev // 2, own_col + cols_dev, own_col - cols_dev)
+    near_row = np.concatenate([own_row + d for d in shifts] + [own_row[:edge] + d for d in shifts])
+    near_col = np.concatenate([own_col] * 3 + [beside[:edge]] * 3)
+    close = (np.abs(near_row[None] - own_row[:, None]) <= RADIUS) & (
+        np.abs(near_col[None] - own_col[:, None]) <= RADIUS
+    )
+    held = lax.axis_index("rows") * rows_dev + jnp.asarray(near_row, jnp.int32)
+    in_grid = ((held >= 0) & (held < grid_rows))[None, :]
+    mask = jnp.where(in_grid, jnp.asarray(close, jnp.float32), 0.0)
+    perm = jnp.asarray(perm, low)
+    payload_width = 4 * inner + STATS
+    vmem = pl.BlockSpec(memory_space=pltpu.VMEM)
+    payload = pl.pallas_call(
+        project_kernel,
+        out_shape=jax.ShapeDtypeStruct((tokens, payload_width), low),
+        in_specs=[vmem] * 7, out_specs=vmem, name="project",
+    )(flat_in, qkv_weight, flat_cot, out_weight, flat_att, log_norm.reshape(HEADS, tokens), perm)
+    dma = pltpu.SemaphoreType.DMA
+    around = pl.pallas_call(
+        functools.partial(halo_kernel, rows_count, edge),
+        out_shape=jax.ShapeDtypeStruct((near, payload_width), low),
+        in_specs=[vmem], out_specs=vmem, name="halo",
+        scratch_shapes=[dma, dma((3, 2)), dma((3, 2)), dma((3,)), dma((3,))],
+        compiler_params=pltpu.CompilerParams(collective_id=1, has_side_effects=True),
+    )(payload)
+    grad_input, partial = pl.pallas_call(
+        attention_kernel,
+        out_shape=(
+            jax.ShapeDtypeStruct((tokens, model_width), low),
+            jax.ShapeDtypeStruct((model_width, 4 * inner), low),
+        ),
+        in_specs=[vmem] * 7, out_specs=(vmem, vmem), name="attention",
+        scratch_shapes=[pltpu.VMEM((tokens, 3 * inner), low)],
+    )(around, mask, perm, flat_in, flat_cot, flat_att, qkv_weight)
+    sums = summed(partial, (tokens * rows_count * lax.axis_size("cols")) ** (-0.5))
+    return (
+        grad_input.reshape(rows_dev, cols_dev, model_width),
+        sums[:, :3 * inner],
+        sums[:, 3 * inner:].T,
+    )
+
+
+def step(inputs, *rest):
+    rows_dev, cols_dev, model_width = inputs.shape
+    fits = (
+        lax.axis_size("cols") == 2 and lax.axis_size("rows") > 2
+        and rows_dev >= RADIUS and cols_dev > 2 * RADIUS and rows_dev * cols_dev % 16 == 0
+        and rows_dev * cols_dev <= 256
+    )
+    return (banded if fits else shards)(inputs, *rest)
+
+
 def solution(mesh):
     in_specs = (
         P("rows", "cols", None),
@@ -290,4 +506,4 @@
         P("rows", "cols", None),
     )
     out_specs = (P("rows", "cols", None), P(), P())
-    return jax.shard_map(shards, mesh=mesh, in_specs=in_specs, out_specs=out_specs, check_vma=False)
+    return jax.shard_map(step, mesh=mesh, in_specs=in_specs, out_specs=out_specs, check_vma=False)

time: 118 us -> 85.4 us (0.72)
  Pallas kernels: 35.2 us -> 73.2 us
  starting transfers between devices: 20.7 us -> 0 us
  local copies, waits for them, and re-layouts: 28.5 us -> 8.38 us
  matrix products: 18.3 us -> 0 us
  waiting for transfers between devices: 6.56 us -> 0 us
  other arithmetic: 7.46 us -> 2.79 us
    pallas_call x0 -> x3, Pallas kernels: none -> 36.3 us  [the longest x1 23.2 us: banded(): pl.pallas_call(functools.partial(halo_kernel, rows_count, edge), out_shap...]
    ppermute x12 -> x0, starting transfers between devices: 20.7 us -> none  [the longest x6 18.7 us: padded(): lax.ppermute(lax.slice_in_dim(block, 0, width, axis=dim), axis, backward)]
    dot_general x10 -> x0, matrix products: 18.3 us -> none  [the longest x1 4.31 us: shards(): jnp.einsum('het,ehd->thd', score_back_grad, near_queries, preferred_eleme...]
    ppermute x12 -> x0, waiting for transfers between devices: 6.56 us -> none  [the longest x6 6.31 us: padded(): lax.ppermute(lax.slice_in_dim(block, block.shape[dim] - width, None, axis...]
    slice x12 -> x2, local copies, waits for them, and re-layouts: 8.17 us -> 2.67 us  [the longest x1 1.41 us: banded(): sums[:, :3 * inner]]
    convert_element_type x5 -> x0, local copies, waits for them, and re-layouts: 5.42 us -> none  [the longest x2 4.9 us: summed(): parts.astype(jnp.bfloat16).reshape(planes, depth, high, 2, half)]
    concatenate x6 -> x0, other arithmetic: 3.42 us -> none  [the longest x4 3.17 us: padded(): block = jnp.concatenate([low, block, high], axis=dim)]
    unnamed x61 -> x5, local copies, waits for them, and re-layouts: 7.7 us -> 4.31 us
  transfers between devices with their start and end apart: 12 -> 0, of which waited for: 5 -> 0; matrix products, arithmetic and copies ran while one was open for 14% -> 0% of each run, Pallas kernels for 0% -> 0%
where the time goes in v2:
time: 85.4 us; the launch traced here: 85 us
  Pallas kernels  73.2 us (86%)
  local copies, waits for them, and re-layouts  8.38 us (10%)
  other arithmetic  2.79 us (3%)
    pallas_call x1, Pallas kernels, summed(): pl.pallas_call(functools.partial(reduce_kernel, planes, depth, width, fac...  36.8 us
    pallas_call x1, Pallas kernels, banded(): pl.pallas_call(functools.partial(halo_kernel, rows_count, edge), out_shap...  23.2 us
    pallas_call x1, Pallas kernels, banded(): pl.pallas_call(attention_kernel, out_shape=(jax.ShapeDtypeStruct((tokens,...  8.95 us
    unnamed x5, local copies, waits for them, and re-layouts  4.31 us
    pallas_call x1, Pallas kernels, banded(): pl.pallas_call(project_kernel, out_shape=jax.ShapeDtypeStruct((tokens, pa...  4.19 us
    select_n x1, other arithmetic, banded(): mask = jnp.where(in_grid, jnp.asarray(close, jnp.float32), 0.0)  1.99 us

profile of v2, /device:TPU:0, one launch (start us, length us, event | category | flops | bytes accessed | tf_op | source)
XLA Modules:
  0.0 85.0 jit_solution(7839559388056218378)
XLA Ops:
  0.6 0.0 copy-start
  0.6 0.8 fusion
  1.4 1.4 %reshape.31.norm_ref = f32[5,192]{1,0:T(8,128)} reshape(f32[5,6,32]{2,1,0:T(8,128)} %param.13) | data formatting | bytes 7680 | tf_op jit(solution)/shard_map/reshape | solution.py:463
  2.8 2.0 %broadcast_select_fusion.mask_ref = f32[192,816]{1,0:T(8,128)} fusion(f32[192,816]{1,0:T(8,128)} %constant.21.clone, pred[816]{0:T(1024)(128)(4,1)S(1)} %fusion), kind=kLoop, calls=%fused_computation | loop fusion | flops 156672 | bytes 1254192 | tf_op jit(solution)/shard_map/jit(_where)/select_n | solution.py:455
  4.8 0.0 copy-done
  4.8 1.9 %copy.12.wqkv_ref = bf16[640,960]{1,0:T(8,128)(2,1)} copy(bf16[640,960]{0,1:T(8,128)(2,1)S(1)} %copy-done) | data formatting | bytes 2457600 | tf_op args[1]
  6.8 4.2 %project.1.x_ref = bf16[192,1408]{1,0:T(8,128)(2,1)} custom-call(bf16[192,640]{1,0:T(8,128)(2,1)} %bitcast.10, bf16[640,960]{1,0:T(8,128)(2,1)} %copy.12.wqkv_ref, bf16[192,640]{1,0:T(8,128)(2,1)} %bitcast.12, bf16[320,640]{1,0:T(8,128)(2,1)} %wout_ref.1, bf16[192,320]{1,0:T(8,128)(2,1)} %bitcast.14, f32[5,192]{1,0:T(8,128)} %reshape.31.norm_ref, ...), custom_call_target="tpu_custom_call" | custom-call | tf_op jit(solution)/shard_map/project/pallas_call | solution.py:459
  11.0 23.2 %halo.1.near_ref = bf16[816,1408]{1,0:T(8,128)(2,1)} custom-call(bf16[192,1408]{1,0:T(8,128)(2,1)} %project.1.x_ref), custom_call_target="tpu_custom_call" | custom-call | tf_op jit(solution)/shard_map/halo/pallas_call | solution.py:465
  34.1 8.9 %attention.1 = (bf16[192,640]{1,0:T(8,128)(2,1)}, bf16[640,1280]{1,0:T(8,128)(2,1)}) custom-call(bf16[816,1408]{1,0:T(8,128)(2,1)} %halo.1.near_ref, f32[192,816]{1,0:T(8,128)} %broadcast_select_fusion.mask_ref, bf16[192,192]{1,0:T(8,128)(2,1)} %constant.22.clone.perm_ref, bf16[192,640]{1,0:T(8,128)(2,1)} %bitcast.11, bf16[192,640]{1,0:T(8,128)(2,1)} %bitcast.13, ...), custom_call_target="tpu_custom_call" | custom-call | tf_op jit(solution)/shard_map/attention/pallas_call | solution.py:472
  43.1 36.8 %weight_sums.1 = bf16[4,4,40,1280]{3,2,1,0:T(8,128)(2,1)} custom-call(bf16[4,4,40,1280]{3,2,1,0:T(8,128)(2,1)} %bitcast.9), custom_call_target="tpu_custom_call" | custom-call | tf_op jit(solution)/shard_map/weight_sums/pallas_call | solution.py:124
  79.9 1.3 %slice.9 = bf16[640,320]{1,0:T(8,128)(2,1)S(1)} slice(bf16[640,1280]{1,0:T(8,128)(2,1)} %bitcast.7), slice={[0:640], [960:1280]} | slice | bytes 819200 | tf_op jit(solution)/shard_map/slice | solution.py:485
  81.2 1.4 %slice.8 = bf16[640,960]{1,0:T(8,128)(2,1)S(1)} slice(bf16[640,1280]{1,0:T(8,128)(2,1)} %bitcast.8), slice={[0:640], [0:960]} | slice | bytes 2457600 | tf_op jit(solution)/shard_map/slice | solution.py:484
  82.6 1.4 %copy.16 = bf16[640,960]{0,1:T(8,128)(2,1)} copy(bf16[640,960]{1,0:T(8,128)(2,1)S(1)} %slice.8) | data formatting | bytes 2457600
  84.0 1.0 %copy.17 = bf16[640,320]{0,1:T(8,128)(2,1)} copy(bf16[640,320]{1,0:T(8,128)(2,1)S(1)} %slice.9) | data formatting | bytes 819200
Async XLA Ops:
  0.6 4.2 %copy-start = (bf16[640,960]{0,1:T(8,128)(2,1)S(1)}, bf16[640,960]{0,1:T(8,128)(2,1)}, u32[]{:S(2)}) copy-start(bf16[640,960]{0,1:T(8,128)(2,1)} %param.10) | copy-start | bytes 3686404

commit v3 on v2

--- a/solution.py
+++ b/solution.py
@@ -17,21 +17,18 @@
 
 
 def reduce_kernel(
-    planes, depth, width, factor,
+    depth, factor,
     x_ref, o_ref, recv1, sum1, recv2, sum2, recv3,
     s1, r1, s2, r2, s3, r3, zs, zr, ps, pr, cs, cr,
 ):
     row, col = lax.axis_index("rows"), lax.axis_index("cols")
     core, lane, z = row % 2, (row // 2) % 2, row // 4
-    p = lane * width + col
     partner = (row + 1 - 2 * core, col)
-    half = x_ref.shape[3] // 2
-    lanes = pl.ds(pl.multiple_of(core * half, 128), half)
-    others = pl.ds(pl.multiple_of((1 - core) * half, 128), half)
-
-    def plane_peer(k):
-        q = (p + k) % planes
-        return q, (z * 4 + (q // width) * 2 + core, q % width)
+
+    def chip(k):
+        y = 1 - lane if k >= 2 else lane
+        x = 1 - col if k % 2 else col
+        return y * 2 + x, (z * 4 + y * 2 + core, x)
 
     def z_peer(k):
         q = (z + k) % depth
@@ -47,97 +44,115 @@
 
     barrier = pltpu.get_barrier_semaphore()
     peers = [partner]
-    peers += [plane_peer(k)[1] for k in range(1, planes)]
+    peers += [chip(k)[1] for k in range(1, 4)]
     peers += [z_peer(k)[1] for k in range(1, depth)]
     for peer in peers:
         pl.semaphore_signal(barrier, inc=1, device_id=peer, device_id_type=MESH)
     pl.semaphore_wait(barrier, len(peers))
 
-    order = list(range(1, planes)) + [0]
-    pair, started = {}, []
-    for k in order:
-        q = (p + k) % planes
-        pair[k] = send(x_ref.at[q, :, :, others], recv1.at[k], s1.at[k], r1.at[k], partner)
-    across = {}
-    for k in order:
-        q, device = plane_peer(k)
+    copies = []
+    pair, across, deep = {}, {}, {}
+    z_order = list(range(1, depth)) + [0]
+    for k in (3, 1, 2, 0):
+        pair[k] = send(
+            x_ref.at[1 - core, chip(k)[0]], recv1.at[k], s1.at[k], r1.at[k], partner
+        )
+    for k in (3, 1, 2, 0):
+        q, device = chip(k)
         pair[k].wait_recv()
-        total = x_ref[q, :, :, lanes].astype(jnp.float32) + recv1[k].astype(jnp.float32)
+        total = x_ref[core, q].astype(jnp.float32) + recv1[k].astype(jnp.float32)
         sum1[k] = total.astype(jnp.bfloat16)
         if k:
-            across[k] = send(sum1.at[k], recv2.at[k - 1], s2.at[k - 1], r2.at[k - 1], device)
-    total = sum1[0].astype(jnp.float32)
-    for k in range(1, planes):
-        across[k].wait_recv()
-        total = total + recv2[k - 1].astype(jnp.float32)
-    sum2[...] = total.astype(jnp.bfloat16)
-    deep = {}
-    for k in range(1, depth):
-        q, device = z_peer(k)
-        deep[k] = send(sum2.at[q], recv3.at[k - 1], s3.at[k - 1], r3.at[k - 1], device)
-    total = sum2[z].astype(jnp.float32)
-    for k in range(1, depth):
-        deep[k].wait_recv()
-        total = total + recv3[k - 1].astype(jnp.float32)
-    o_ref[p, z, :, lanes] = (total * factor).astype(jnp.bfloat16)
-
-    own = o_ref.at[p, z, :, lanes]
-    zcopies, pcopies = {}, {}
+            for kz in z_order:
+                across[k, kz] = send(
+                    sum1.at[k, z_peer(kz)[0]], recv2.at[k - 1, kz],
+                    s2.at[k - 1, kz], r2.at[k - 1, kz], device,
+                )
+    for kz in z_order:
+        q, device = z_peer(kz)
+        total = sum1[0, q].astype(jnp.float32)
+        for k in range(1, 4):
+            across[k, kz].wait_recv()
+            total = total + recv2[k - 1, kz].astype(jnp.float32)
+        if kz:
+            sum2[kz - 1] = total.astype(jnp.bfloat16)
+            deep[kz] = send(
+                sum2.at[kz - 1], recv3.at[kz - 1], s3.at[kz - 1], r3.at[kz - 1], device
+            )
+    for kz in range(1, depth):
+        deep[kz].wait_recv()
+        total = total + recv3[kz - 1].astype(jnp.float32)
+    o_ref[core, chip(0)[0], z] = (total * factor).astype(jnp.bfloat16)
+
+    def piece(k, kz):
+        return o_ref.at[core, chip(k)[0], (z - kz + depth) % depth]
+
+    zcopies, pcopies, started = {}, {}, []
+
+    def forward(k, kz):
+        started.append(send(piece(k, kz), piece(k, kz), cs.at[k, kz], cr.at[k, kz], partner))
+
+    def share(kz):
+        for k in (1, 2):
+            pcopies[k, kz] = send(
+                piece(0, kz), piece(0, kz), ps.at[k - 1, kz], pr.at[k - 1, kz], chip(k)[1]
+            )
+        forward(0, kz)
+
+    own = piece(0, 0)
     for k in range(1, depth):
         zcopies[k] = send(own, own, zs.at[k - 1], zr.at[k - 1], z_peer(k)[1])
-
-    def share(kz, piece):
-        for k in range(1, planes):
-            pcopies[k, kz] = send(
-                piece, piece, ps.at[k - 1, kz], pr.at[k - 1, kz], plane_peer(k)[1]
-            )
-        started.append(send(piece, piece, cs.at[0, kz], cr.at[0, kz], partner))
-
-    share(0, own)
+    share(0)
     for k in range(1, depth):
         zcopies[k].wait_recv()
-        share(k, o_ref.at[p, (z - k + depth) % depth, :, lanes])
+        share(k)
     for kz in range(depth):
-        for k in range(1, planes):
+        via = 1 + kz % 2
+        for k in (via, 3 - via):
             pcopies[k, kz].wait_recv()
-            piece = o_ref.at[(p - k + planes) % planes, (z - kz + depth) % depth, :, lanes]
-            started.append(send(piece, piece, cs.at[k, kz], cr.at[k, kz], partner))
+            if k == via:
+                pcopies[3, kz] = send(
+                    piece(k, kz), piece(k, kz), ps.at[2, kz], pr.at[2, kz], chip(3 - k)[1]
+                )
+            forward(k, kz)
+    for kz in range(depth):
+        pcopies[3, kz].wait_recv()
+        forward(3, kz)
     for copy in started:
         copy.wait_recv()
-    for copy in [*started, *pair.values(), *across.values(), *deep.values(),
-                 *zcopies.values(), *pcopies.values()]:
+    copies = [pair, across, deep, zcopies, pcopies]
+    for copy in [c for group in copies for c in group.values()] + started:
         copy.wait_send()
 
 
 def summed(parts, factor):
-    rows = parts.shape[0]
-    columns = parts.shape[1]
+    rows, columns = parts.shape
     count, width = lax.axis_size("rows"), lax.axis_size("cols")
-    planes, depth = 2 * width, max(count // 4, 1)
-    half = columns // 2
-    if count % 4 or rows % (planes * depth * 8) or columns % 256 or depth < 2:
-        return (lax.psum(parts.astype(jnp.float32), ("rows", "cols")) * factor).astype(jnp.bfloat16)
-    high = rows // (planes * depth)
-    x = parts.astype(jnp.bfloat16).reshape(planes, depth, high, columns)
+    depth = count // 4
+    if width != 2 or count % 4 or depth < 2 or rows % (64 * depth) or columns % 128:
+        total = lax.psum(parts.astype(jnp.float32), ("rows", "cols"))
+        return (total * factor).astype(jnp.bfloat16)
+    high = rows // (8 * depth)
     low = jnp.bfloat16
+    x = parts.astype(low).reshape(2, 4, depth, high, columns)
     dma = pltpu.SemaphoreType.DMA
     out = pl.pallas_call(
-        functools.partial(reduce_kernel, planes, depth, width, factor),
-        out_shape=jax.ShapeDtypeStruct((planes, depth, high, columns), low),
+        functools.partial(reduce_kernel, depth, factor),
+        out_shape=jax.ShapeDtypeStruct(x.shape, low),
         in_specs=[pl.BlockSpec(memory_space=pltpu.VMEM)],
         out_specs=pl.BlockSpec(memory_space=pltpu.VMEM),
         scratch_shapes=[
-            pltpu.VMEM((planes, depth, high, half), low),
-            pltpu.VMEM((planes, depth, high, half), low),
-            pltpu.VMEM((planes - 1, depth, high, half), low),
-            pltpu.VMEM((depth, high, half), low),
-            pltpu.VMEM((depth - 1, high, half), low),
-            dma((planes,)), dma((planes,)),
-            dma((planes - 1,)), dma((planes - 1,)),
+            pltpu.VMEM((4, depth, high, columns), low),
+            pltpu.VMEM((4, depth, high, columns), low),
+            pltpu.VMEM((3, depth, high, columns), low),
+            pltpu.VMEM((depth - 1, high, columns), low),
+            pltpu.VMEM((depth - 1, high, columns), low),
+            dma((4,)), dma((4,)),
+            dma((3, depth)), dma((3, depth)),
             dma((depth - 1,)), dma((depth - 1,)),
             dma((depth - 1,)), dma((depth - 1,)),
-            dma((planes - 1, depth)), dma((planes - 1, depth)),
-            dma((planes, depth)), dma((planes, depth)),
+            dma((3, depth)), dma((3, depth)),
+            dma((4, depth)), dma((4, depth)),
         ],
         compiler_params=pltpu.CompilerParams(collective_id=0, has_side_effects=True),
         name="weight_sums",
@@ -195,7 +210,7 @@
         flat_cot, out_weight, (((1,), (1,)), ((), ())), preferred_element_type=jnp.float32
     ).astype(jnp.bfloat16)
     grad_wout = lax.dot_general(
-        flat_cot, flat_att, (((0,), (0,)), ((), ())), preferred_element_type=jnp.float32
+        flat_att, flat_cot, (((0,), (0,)), ((), ())), preferred_element_type=jnp.float32
     )
     head_shape = (tokens_dev, HEADS, HEAD_DIM)
     queries = projected[:, :inner_width].reshape(head_shape)
@@ -279,9 +294,9 @@
     grad_wqkv = lax.dot_general(
         flat_in, grad_proj, (((0,), (0,)), ((), ())), preferred_element_type=jnp.float32
     )
-    sums = summed(jnp.concatenate([grad_wqkv, grad_wout], axis=1), grad_factor)
+    sums = summed(jnp.concatenate([grad_wqkv.T, grad_wout], axis=0), grad_factor)
     columns = grad_wqkv.shape[1]
-    return grad_input, sums[:, :columns], sums[:, columns:].T
+    return grad_input, sums[:columns].T, sums[columns:]
 
 
 STATS = 128
@@ -303,13 +318,13 @@
     tokens, inner = att_ref.shape
     low = jnp.bfloat16
     perm = perm_ref[...]
-    projected = dot(in_ref[...], wqkv_ref[...]).astype(low)
+    projected = dot(in_ref[...], wqkv_ref[...], NT).astype(low)
     upstream = dot(cot_ref[...], wout_ref[...], NT).astype(low)
     width = 3 * inner
     product = upstream.astype(jnp.float32) * att_ref[...].astype(jnp.float32)
     lane = lax.broadcasted_iota(jnp.int32, (tokens, STATS), 1)
     stats = jnp.zeros((tokens, STATS), jnp.float32)
-    norm = norm_ref[...]
+    norm = jnp.concatenate([norm_ref[:, r] for r in range(norm_ref.shape[1])], axis=1)
     norm_high, norm_low = terms(norm)
     norm_high, norm_low = dot(perm, norm_high.astype(low), NT), dot(perm, norm_low.astype(low), NT)
     for h in range(HEADS):
@@ -375,12 +390,18 @@
 
 
 def attention_kernel(
-    near_ref, mask_ref, perm_ref, in_ref, cot_ref, att_ref, wqkv_ref, gin_ref, part_ref, grads,
+    rows_count, near_ref, mask_ref, perm_ref, in_ref, cot_ref, att_ref, wqkv_ref, gin_ref, part_ref, grads,
 ):
     tokens, inner = att_ref.shape
     low = jnp.bfloat16
     scale = HEAD_DIM ** (-0.5)
-    inside = mask_ref[...] > 0.5
+    row = lax.axis_index("rows")
+    at = lax.broadcasted_iota(jnp.int32, mask_ref.shape, 1)
+    edge = mask_ref.shape[1] // 3 - tokens
+    above = (at < tokens) | ((at >= 3 * tokens) & (at < 3 * tokens + edge))
+    below = ((at >= 2 * tokens) & (at < 3 * tokens)) | (at >= 3 * tokens + 2 * edge)
+    outside = (above & (row == 0)) | (below & (row == rows_count - 1))
+    inside = (mask_ref[...].astype(jnp.float32) > 0.5) & jnp.logical_not(outside)
     own = pl.ds(tokens, tokens)
     width = 4 * inner
     near_stats = near_ref[:, width:]
@@ -419,9 +440,9 @@
             at = block * inner + h * HEAD_DIM
             grads[:, at:at + HEAD_DIM] = grad.astype(low)
     grad_proj = dot(perm_ref[...], grads[...], TN).astype(low)
-    gin_ref[...] = dot(grad_proj, wqkv_ref[...], NT).astype(low)
-    part_ref[:, :3 * inner] = dot(in_ref[...], grad_proj, TN).astype(low)
-    part_ref[:, 3 * inner:] = dot(cot_ref[...], att_ref[...], TN).astype(low)
+    gin_ref[...] = dot(grad_proj, wqkv_ref[...]).astype(low)
+    part_ref[:3 * inner] = dot(grad_proj, in_ref[...], TN).astype(low)
+    part_ref[3 * inner:] = dot(att_ref[...], cot_ref[...], TN).astype(low)
 
 
 def banded(inputs, qkv_weight, out_weight, attn_out, log_norm, cotangent):
@@ -429,7 +450,6 @@
     tokens = rows_dev * cols_dev
     inner = HEADS * HEAD_DIM
     rows_count = lax.axis_size("rows")
-    grid_rows = rows_count * rows_dev
     edge = -(-2 * RADIUS * rows_dev // 16) * 16
     near = 3 * (tokens + edge)
     low = jnp.bfloat16
@@ -450,17 +470,16 @@
     close = (np.abs(near_row[None] - own_row[:, None]) <= RADIUS) & (
         np.abs(near_col[None] - own_col[:, None]) <= RADIUS
     )
-    held = lax.axis_index("rows") * rows_dev + jnp.asarray(near_row, jnp.int32)
-    in_grid = ((held >= 0) & (held < grid_rows))[None, :]
-    mask = jnp.where(in_grid, jnp.asarray(close, jnp.float32), 0.0)
+    mask = jnp.asarray(close, low)
     perm = jnp.asarray(perm, low)
+    wqkv = qkv_weight.T
     payload_width = 4 * inner + STATS
     vmem = pl.BlockSpec(memory_space=pltpu.VMEM)
     payload = pl.pallas_call(
         project_kernel,
         out_shape=jax.ShapeDtypeStruct((tokens, payload_width), low),
         in_specs=[vmem] * 7, out_specs=vmem, name="project",
-    )(flat_in, qkv_weight, flat_cot, out_weight, flat_att, log_norm.reshape(HEADS, tokens), perm)
+    )(flat_in, wqkv, flat_cot, out_weight, flat_att, log_norm, perm)
     dma = pltpu.SemaphoreType.DMA
     around = pl.pallas_call(
         functools.partial(halo_kernel, rows_count, edge),
@@ -470,19 +489,19 @@
         compiler_params=pltpu.CompilerParams(collective_id=1, has_side_effects=True),
     )(payload)
     grad_input, partial = pl.pallas_call(
-        attention_kernel,
+        functools.partial(attention_kernel, rows_count),
         out_shape=(
             jax.ShapeDtypeStruct((tokens, model_width), low),
-            jax.ShapeDtypeStruct((model_width, 4 * inner), low),
+            jax.ShapeDtypeStruct((4 * inner, model_width), low),
         ),
         in_specs=[vmem] * 7, out_specs=(vmem, vmem), name="attention",
         scratch_shapes=[pltpu.VMEM((tokens, 3 * inner), low)],
-    )(around, mask, perm, flat_in, flat_cot, flat_att, qkv_weight)
+    )(around, mask, perm, flat_in, flat_cot, flat_att, wqkv)
     sums = summed(partial, (tokens * rows_count * lax.axis_size("cols")) ** (-0.5))
     return (
         grad_input.reshape(rows_dev, cols_dev, model_width),
-        sums[:, :3 * inner],
-        sums[:, 3 * inner:].T,
+        sums[:3 * inner].T,
+        sums[3 * inner:],
     )
 
 

time: 85.4 us -> 76.7 us (0.90)
  local copies, waits for them, and re-layouts: 8.38 us -> 4.21 us
  other arithmetic: 2.79 us -> 0 us
  Pallas kernels: 73.2 us -> 71.6 us
    unnamed x5 -> x0, local copies, waits for them, and re-layouts: 4.31 us -> none
    transpose x0 -> x1, local copies, waits for them, and re-layouts: none -> 2.42 us  [banded(): sums[:3 * inner]]
    select_n x1 -> x0, other arithmetic: 1.99 us -> none  [banded(): mask = jnp.where(in_grid, jnp.asarray(close, jnp.float32), 0.0)]
    pallas_call x2, Pallas kernels: 45.8 us -> 44.2 us  [the longest x1 35.4 us: summed(): pl.pallas_call(functools.partial(reduce_kernel, depth, factor), out_shape...]
    reshape x1 -> x0, local copies, waits for them, and re-layouts: 1.4 us -> none  [banded(): log_norm.reshape(HEADS, tokens)]
    slice x2 -> x1, local copies, waits for them, and re-layouts: 2.67 us -> 1.79 us  [banded(): sums[3 * inner:]]
where the time goes in v3:
time: 76.7 us; the launch traced here: 76.4 us
  Pallas kernels  71.6 us (93%)
  local copies, waits for them, and re-layouts  4.21 us (5%)
    pallas_call x1, Pallas kernels, summed(): pl.pallas_call(functools.partial(reduce_kernel, depth, factor), out_shape...  35.4 us
    pallas_call x1, Pallas kernels, banded(): pl.pallas_call(functools.partial(halo_kernel, rows_count, edge), out_shap...  23.2 us
    pallas_call x1, Pallas kernels, banded(): pl.pallas_call(functools.partial(attention_kernel, rows_count), out_shape...  8.76 us
    pallas_call x1, Pallas kernels, banded(): pl.pallas_call(project_kernel, out_shape=jax.ShapeDtypeStruct((tokens, pa...  4.21 us
    transpose x1, local copies, waits for them, and re-layouts, banded(): sums[:3 * inner]  2.42 us
    slice x1, local copies, waits for them, and re-layouts, banded(): sums[3 * inner:]  1.79 us

profile of v3, /device:TPU:0, one launch (start us, length us, event | category | flops | bytes accessed | tf_op | source)
XLA Modules:
  0.0 76.4 jit_solution(18363316714797238413)
XLA Ops:
  0.6 4.2 %project.1.x_ref = bf16[192,1408]{1,0:T(8,128)(2,1)} custom-call(bf16[192,640]{1,0:T(8,128)(2,1)} %bitcast.14, bf16[960,640]{1,0:T(8,128)(2,1)} %bitcast.11, bf16[192,640]{1,0:T(8,128)(2,1)} %bitcast.16, bf16[320,640]{1,0:T(8,128)(2,1)} %wout_ref.1, bf16[192,320]{1,0:T(8,128)(2,1)} %bitcast.18, f32[5,6,32]{2,1,0:T(8,128)} %norm_ref.1, ...), custom_call_target="tpu_custom_call" | custom-call | tf_op jit(solution)/shard_map/project/pallas_call | solution.py:478
  4.8 23.2 %halo.1.near_ref = bf16[816,1408]{1,0:T(8,128)(2,1)} custom-call(bf16[192,1408]{1,0:T(8,128)(2,1)} %project.1.x_ref), custom_call_target="tpu_custom_call" | custom-call | tf_op jit(solution)/shard_map/halo/pallas_call | solution.py:484
  28.0 8.8 %attention.1 = (bf16[192,640]{1,0:T(8,128)(2,1)}, bf16[1280,640]{1,0:T(8,128)(2,1)}) custom-call(bf16[816,1408]{1,0:T(8,128)(2,1)} %halo.1.near_ref, bf16[192,816]{1,0:T(8,128)(2,1)} %constant.4.clone.mask_ref, bf16[192,192]{1,0:T(8,128)(2,1)} %constant.5.clone.perm_ref, bf16[192,640]{1,0:T(8,128)(2,1)} %bitcast.15, bf16[192,640]{1,0:T(8,128)(2,1)} %bitcast.17, ...), custom_call_target="tpu_custom_call" | custom-call | tf_op jit(solution)/shard_map/attention/pallas_call | solution.py:491
  36.8 35.4 %weight_sums.1 = bf16[2,4,4,40,640]{4,3,2,1,0:T(8,128)(2,1)} custom-call(bf16[2,4,4,40,640]{4,3,2,1,0:T(8,128)(2,1)} %bitcast.13), custom_call_target="tpu_custom_call" | custom-call | tf_op jit(solution)/shard_map/weight_sums/pallas_call | solution.py:139
  72.2 1.8 %slice.9 = bf16[320,640]{1,0:T(8,128)(2,1)} slice(bf16[1280,640]{1,0:T(8,128)(2,1)} %bitcast.9), slice={[960:1280], [0:640]} | slice | bytes 819200 | tf_op jit(solution)/shard_map/slice | solution.py:504
  74.0 2.4 %slice_bitcast_fusion = bf16[640,960]{0,1:T(8,128)(2,1)} fusion(bf16[1280,640]{1,0:T(8,128)(2,1)} %bitcast.10), kind=kLoop, calls=%fused_computation | loop fusion | bytes 2457600 | tf_op jit(solution)/shard_map/transpose | solution.py:503

commit v4 on v3

--- a/solution.py
+++ b/solution.py
@@ -341,52 +341,107 @@
     o_ref[:, width + inner:] = moved.astype(low)
 
 
-def halo_kernel(rows_count, edge, x_ref, o_ref, own_sem, rs, rr, xs, xr):
+def halo_kernel(rows_count, edge, x_ref, o_ref, own_sem, rs, rr):
     row, col = lax.axis_index("rows"), lax.axis_index("cols")
+    core = row % 2
     tokens = x_ref.shape[0]
-    above = ((row + rows_count - 1) % rows_count, col)
-    below = ((row + 1) % rows_count, col)
     beside = (row, 1 - col)
-
-    def send(src, dst, ssem, rsem, device):
-        copy = pltpu.make_async_remote_copy(
-            src_ref=src, dst_ref=dst, send_sem=ssem, recv_sem=rsem,
+    partner = (row + 1 - 2 * core, col)
+    far = (row - 1 + 2 * core, col)
+    inner_end = (row > 0) & (row < rows_count - 1)
+    barrier = pltpu.get_barrier_semaphore()
+
+    def greet(device):
+        pl.semaphore_signal(barrier, inc=1, device_id=device, device_id_type=MESH)
+
+    def remote(src, dst, n, device):
+        return pltpu.make_async_remote_copy(
+            src_ref=src, dst_ref=dst, send_sem=rs.at[n], recv_sem=rr.at[n],
             device_id=device, device_id_type=MESH,
         )
-        copy.start()
-        return copy
-
-    barrier = pltpu.get_barrier_semaphore()
-    for peer in (above, below, beside):
-        pl.semaphore_signal(barrier, inc=1, device_id=peer, device_id_type=MESH)
-    pl.semaphore_wait(barrier, 3)
 
     def band(slot, first, size):
-        return o_ref.at[pl.ds(slot * tokens + first, size), :]
+        return o_ref.at[pl.ds(pl.multiple_of(slot * tokens + first, 16), size), :]
 
     def side(slot):
-        return o_ref.at[pl.ds(3 * tokens + slot * edge, edge), :]
+        return o_ref.at[pl.ds(pl.multiple_of(3 * tokens + slot * edge, 16), edge), :]
 
     rest = tokens - edge
     head, tail = x_ref.at[pl.ds(0, edge), :], x_ref.at[pl.ds(edge, rest), :]
-    first = {}
-    for slot, device in ((2, above), (0, below)):
-        first[slot] = send(head, band(slot, 0, edge), rs.at[slot, 0], rr.at[slot, 0], device)
-    copies = [send(head, side(1), xs.at[1], xr.at[1], beside)]
-    for slot, device in ((2, above), (0, below)):
-        copies.append(
-            send(tail, band(slot, edge, rest), rs.at[slot, 1], rr.at[slot, 1], device)
-        )
+    far_slot = 2 * core
+    near_slot = 2 - far_slot
+
+    @pl.when(inner_end)
+    def _():
+        greet(far)
+
+    greet(partner)
+    greet(beside)
+    pl.semaphore_wait(barrier, 2 + inner_end.astype(jnp.int32))
+
+    far_head = remote(head, band(near_slot, 0, edge), 0, far)
+    far_tail = remote(tail, band(near_slot, edge, rest), 1, far)
+    side_own = remote(head, side(1), 2, beside)
+    pair_head = remote(x_ref, band(far_slot, 0, tokens), 3, partner)
+    side_far = remote(band(far_slot, 0, edge), side(far_slot), 4, beside)
+    side_pair = remote(side(1), side(far_slot), 5, partner)
+
+    @pl.when(inner_end)
+    def _():
+        far_head.start()
+
+    side_own.start()
+
+    @pl.when(inner_end)
+    def _():
+        far_tail.start()
+
+    pair_head.start()
     own = pltpu.make_async_copy(x_ref, band(1, 0, tokens), own_sem)
     own.start()
-    for slot in (0, 2):
-        first[slot].wait_recv()
-        copies.append(send(band(slot, 0, edge), side(slot), xs.at[slot], xr.at[slot], beside))
+
+    @pl.when(jnp.logical_not(inner_end))
+    def _():
+        for view in (band(far_slot, 0, tokens), side(far_slot)):
+            view[...] = jnp.zeros(view.shape, view.dtype)
+
+    side_own.wait_recv()
+    side_pair.start()
+
+    @pl.when(inner_end)
+    def _():
+        far_head.wait_recv()
+        side_far.start()
+
+    pair_head.wait_recv()
+    side_pair.wait_recv()
+
+    @pl.when(inner_end)
+    def _():
+        far_tail.wait_recv()
+        side_far.wait_recv()
+        far_head.wait_send()
+        far_tail.wait_send()
+        side_far.wait_send()
+
+    side_own.wait_send()
+    pair_head.wait_send()
+    side_pair.wait_send()
+    own.wait()
+
+
+def split_kernel(x_ref, a_ref, b_ref, sems):
+    rows = a_ref.shape[0]
+    half = rows // 2
+    copies = [
+        pltpu.make_async_copy(x_ref.at[pl.ds(0, half)], a_ref.at[pl.ds(0, half)], sems.at[0]),
+        pltpu.make_async_copy(x_ref.at[pl.ds(half, half)], a_ref.at[pl.ds(half, half)], sems.at[1]),
+        pltpu.make_async_copy(x_ref.at[pl.ds(rows, b_ref.shape[0])], b_ref, sems.at[2]),
+    ]
     for copy in copies:
-        copy.wait_recv()
-    for copy in [*copies, *first.values()]:
-        copy.wait_send()
-    own.wait()
+        copy.start()
+    for copy in copies:
+        copy.wait()
 
 
 def attention_kernel(
@@ -485,7 +540,7 @@
         functools.partial(halo_kernel, rows_count, edge),
         out_shape=jax.ShapeDtypeStruct((near, payload_width), low),
         in_specs=[vmem], out_specs=vmem, name="halo",
-        scratch_shapes=[dma, dma((3, 2)), dma((3, 2)), dma((3,)), dma((3,))],
+        scratch_shapes=[dma, dma((6,)), dma((6,))],
         compiler_params=pltpu.CompilerParams(collective_id=1, has_side_effects=True),
     )(payload)
     grad_input, partial = pl.pallas_call(
@@ -498,17 +553,27 @@
         scratch_shapes=[pltpu.VMEM((tokens, 3 * inner), low)],
     )(around, mask, perm, flat_in, flat_cot, flat_att, wqkv)
     sums = summed(partial, (tokens * rows_count * lax.axis_size("cols")) ** (-0.5))
+    anywhere = pl.BlockSpec(memory_space=pl.ANY)
+    grad_wqkv, grad_wout = pl.pallas_call(
+        split_kernel,
+        out_shape=(
+            jax.ShapeDtypeStruct((3 * inner, model_width), low),
+            jax.ShapeDtypeStruct((inner, model_width), low),
+        ),
+        in_specs=[vmem], out_specs=(anywhere, anywhere), name="split",
+        scratch_shapes=[dma((3,))],
+    )(sums)
     return (
         grad_input.reshape(rows_dev, cols_dev, model_width),
-        sums[:3 * inner].T,
-        sums[3 * inner:],
+        grad_wqkv.T,
+        grad_wout,
     )
 
 
 def step(inputs, *rest):
     rows_dev, cols_dev, model_width = inputs.shape
     fits = (
-        lax.axis_size("cols") == 2 and lax.axis_size("rows") > 2
+        lax.axis_size("cols") == 2 and lax.axis_size("rows") % 2 == 0
         and rows_dev >= RADIUS and cols_dev > 2 * RADIUS and rows_dev * cols_dev % 16 == 0
         and rows_dev * cols_dev <= 256
     )

time: 76.7 us -> 72.2 us (0.941)
  local copies, waits for them, and re-layouts: 4.21 us -> 0 us
    pallas_call x1, Pallas kernels: 23.2 us -> 12.7 us  [banded(): pl.pallas_call(functools.partial(halo_kernel, rows_count, edge), out_shap...]
    pallas_call x1, Pallas kernels: 35.4 us -> 43 us  [summed(): pl.pallas_call(functools.partial(reduce_kernel, depth, factor), out_shape...]
    pallas_call x0 -> x1, Pallas kernels: none -> 2.61 us  [banded(): pl.pallas_call(split_kernel, out_shape=(jax.ShapeDtypeStruct((3 * inner,...]
    transpose x1 -> x0, local copies, waits for them, and re-layouts: 2.42 us -> none  [banded(): sums[:3 * inner]]
    slice x1 -> x0, local copies, waits for them, and re-layouts: 1.79 us -> none  [banded(): sums[3 * inner:]]
where the time goes in v4:
time: 72.2 us; the launch traced here: 71.9 us
  Pallas kernels  71.3 us (99%)
    pallas_call x1, Pallas kernels, summed(): pl.pallas_call(functools.partial(reduce_kernel, depth, factor), out_shape...  43 us
    pallas_call x1, Pallas kernels, banded(): pl.pallas_call(functools.partial(halo_kernel, rows_count, edge), out_shap...  12.7 us
    pallas_call x1, Pallas kernels, banded(): pl.pallas_call(functools.partial(attention_kernel, rows_count), out_shape...  8.75 us
    pallas_call x1, Pallas kernels, banded(): pl.pallas_call(project_kernel, out_shape=jax.ShapeDtypeStruct((tokens, pa...  4.21 us
    pallas_call x1, Pallas kernels, banded(): pl.pallas_call(split_kernel, out_shape=(jax.ShapeDtypeStruct((3 * inner,...  2.61 us

profile of v4, /device:TPU:0, one launch (start us, length us, event | category | flops | bytes accessed | tf_op | source)
XLA Modules:
  0.0 71.9 jit_solution(7927819023440962497)
XLA Ops:
  0.6 4.2 %project.1.x_ref = bf16[192,1408]{1,0:T(8,128)(2,1)} custom-call(bf16[192,640]{1,0:T(8,128)(2,1)} %bitcast.12, bf16[960,640]{1,0:T(8,128)(2,1)} %bitcast.9, bf16[192,640]{1,0:T(8,128)(2,1)} %bitcast.14, bf16[320,640]{1,0:T(8,128)(2,1)} %wout_ref.1, bf16[192,320]{1,0:T(8,128)(2,1)} %bitcast.16, f32[5,6,32]{2,1,0:T(8,128)} %norm_ref.1, ...), custom_call_target="tpu_custom_call" | custom-call | tf_op jit(solution)/shard_map/project/pallas_call | solution.py:533
  4.8 12.7 %halo.1.near_ref = bf16[816,1408]{1,0:T(8,128)(2,1)} custom-call(bf16[192,1408]{1,0:T(8,128)(2,1)} %project.1.x_ref), custom_call_target="tpu_custom_call" | custom-call | tf_op jit(solution)/shard_map/halo/pallas_call | solution.py:539
  17.5 8.7 %attention.1 = (bf16[192,640]{1,0:T(8,128)(2,1)}, bf16[1280,640]{1,0:T(8,128)(2,1)}) custom-call(bf16[816,1408]{1,0:T(8,128)(2,1)} %halo.1.near_ref, bf16[192,816]{1,0:T(8,128)(2,1)} %constant.4.clone.mask_ref, bf16[192,192]{1,0:T(8,128)(2,1)} %constant.5.clone.perm_ref, bf16[192,640]{1,0:T(8,128)(2,1)} %bitcast.13, bf16[192,640]{1,0:T(8,128)(2,1)} %bitcast.15, ...), custom_call_target="tpu_custom_call" | custom-call | tf_op jit(solution)/shard_map/attention/pallas_call | solution.py:546
  26.3 43.0 %weight_sums.1 = bf16[2,4,4,40,640]{4,3,2,1,0:T(8,128)(2,1)} custom-call(bf16[2,4,4,40,640]{4,3,2,1,0:T(8,128)(2,1)} %bitcast.11), custom_call_target="tpu_custom_call" | custom-call | tf_op jit(solution)/shard_map/weight_sums/pallas_call | solution.py:139
  69.3 2.6 %split.1 = (bf16[960,640]{1,0:T(8,128)(2,1)}, bf16[320,640]{1,0:T(8,128)(2,1)}) custom-call(bf16[1280,640]{1,0:T(8,128)(2,1)} %bitcast.8), custom_call_target="tpu_custom_call" | custom-call | tf_op jit(solution)/shard_map/split/pallas_call | solution.py:557

commit v5 on v4

--- a/solution.py
+++ b/solution.py
@@ -154,7 +154,7 @@
             dma((3, depth)), dma((3, depth)),
             dma((4, depth)), dma((4, depth)),
         ],
-        compiler_params=pltpu.CompilerParams(collective_id=0, has_side_effects=True),
+        compiler_params=pltpu.CompilerParams(collective_id=0, has_side_effects=True, vmem_limit_bytes=GRANT),
         name="weight_sums",
     )(x)
     return out.reshape(rows, columns)
@@ -300,6 +300,7 @@
 
 
 STATS = 128
+GRANT = 32 * 1024 * 1024
 NT = (((1,), (1,)), ((), ()))
 NN = (((1,), (0,)), ((), ()))
 TN = (((0,), (0,)), ((), ()))
@@ -534,6 +535,7 @@
         project_kernel,
         out_shape=jax.ShapeDtypeStruct((tokens, payload_width), low),
         in_specs=[vmem] * 7, out_specs=vmem, name="project",
+        compiler_params=pltpu.CompilerParams(vmem_limit_bytes=GRANT),
     )(flat_in, wqkv, flat_cot, out_weight, flat_att, log_norm, perm)
     dma = pltpu.SemaphoreType.DMA
     around = pl.pallas_call(
@@ -541,7 +543,7 @@
         out_shape=jax.ShapeDtypeStruct((near, payload_width), low),
         in_specs=[vmem], out_specs=vmem, name="halo",
         scratch_shapes=[dma, dma((6,)), dma((6,))],
-        compiler_params=pltpu.CompilerParams(collective_id=1, has_side_effects=True),
+        compiler_params=pltpu.CompilerParams(collective_id=1, has_side_effects=True, vmem_limit_bytes=GRANT),
     )(payload)
     grad_input, partial = pl.pallas_call(
         functools.partial(attention_kernel, rows_count),
@@ -551,6 +553,7 @@
         ),
         in_specs=[vmem] * 7, out_specs=(vmem, vmem), name="attention",
         scratch_shapes=[pltpu.VMEM((tokens, 3 * inner), low)],
+        compiler_params=pltpu.CompilerParams(vmem_limit_bytes=GRANT),
     )(around, mask, perm, flat_in, flat_cot, flat_att, wqkv)
     sums = summed(partial, (tokens * rows_count * lax.axis_size("cols")) ** (-0.5))
     anywhere = pl.BlockSpec(memory_space=pl.ANY)
@@ -562,6 +565,7 @@
         ),
         in_specs=[vmem], out_specs=(anywhere, anywhere), name="split",
         scratch_shapes=[dma((3,))],
+        compiler_params=pltpu.CompilerParams(vmem_limit_bytes=GRANT),
     )(sums)
     return (
         grad_input.reshape(rows_dev, cols_dev, model_width),

time: 72.2 us -> 67 us (0.928)
  Pallas kernels: 71.3 us -> 59.2 us
  local copies, waits for them, and re-layouts: 0 us -> 6.73 us
    unnamed x0 -> x22, local copies, waits for them, and re-layouts: none -> 6.73 us
    pallas_call x1, Pallas kernels: 8.75 us -> 5.43 us  [banded(): pl.pallas_call(functools.partial(attention_kernel, rows_count), out_shape...]
    pallas_call x1, Pallas kernels: 43 us -> 40.4 us  [summed(): pl.pallas_call(functools.partial(reduce_kernel, depth, factor), out_shape...]
    pallas_call x1, Pallas kernels: 4.21 us -> 1.81 us  [banded(): pl.pallas_call(project_kernel, out_shape=jax.ShapeDtypeStruct((tokens, pa...]
    pallas_call x1, Pallas kernels: 12.7 us -> 10.3 us  [banded(): pl.pallas_call(functools.partial(halo_kernel, rows_count, edge), out_shap...]
    pallas_call x1, Pallas kernels: 2.61 us -> 1.19 us  [banded(): pl.pallas_call(split_kernel, out_shape=(jax.ShapeDtypeStruct((3 * inner,...]
where the time goes in v5:
time: 67 us; the launch traced here: 66.6 us
  Pallas kernels  59.2 us (88%)
  local copies, waits for them, and re-layouts  6.73 us (10%)
  between operations  0.73 us (1%)
    pallas_call x1, Pallas kernels, summed(): pl.pallas_call(functools.partial(reduce_kernel, depth, factor), out_shape...  40.4 us
    pallas_call x1, Pallas kernels, banded(): pl.pallas_call(functools.partial(halo_kernel, rows_count, edge), out_shap...  10.3 us
    unnamed x22, local copies, waits for them, and re-layouts  6.73 us
    pallas_call x1, Pallas kernels, banded(): pl.pallas_call(functools.partial(attention_kernel, rows_count), out_shape...  5.43 us
    pallas_call x1, Pallas kernels, banded(): pl.pallas_call(project_kernel, out_shape=jax.ShapeDtypeStruct((tokens, pa...  1.81 us

profile of v5, /device:TPU:0, one launch (start us, length us, event | category | flops | bytes accessed | tf_op | source)
XLA Modules:
  0.0 66.6 jit_solution(8392283079275369609)
XLA Ops:
  0.6 0.0 copy-start
  0.6 1.3 %copy-done = bf16[640,960]{0,1:T(8,128)(2,1)S(1)} copy-done((bf16[640,960]{0,1:T(8,128)(2,1)S(1)}, bf16[640,960]{0,1:T(8,128)(2,1)}, u32[]{:S(2)}) %copy-start) | copy-done | bytes 1228824
  1.9 0.0 copy-start.2
  1.9 0.9 %copy-done.2 = bf16[6,32,640]{2,1,0:T(8,128)(2,1)S(1)} copy-done((bf16[6,32,640]{2,1,0:T(8,128)(2,1)S(1)}, bf16[6,32,640]{2,1,0:T(8,128)(2,1)}, u32[]{:S(2)}) %copy-start.2) | copy-done | bytes 245784
  2.9 0.0 copy-start.3
  2.9 0.9 %copy-done.3 = bf16[6,32,640]{2,1,0:T(8,128)(2,1)S(1)} copy-done((bf16[6,32,640]{2,1,0:T(8,128)(2,1)S(1)}, bf16[6,32,640]{2,1,0:T(8,128)(2,1)}, u32[]{:S(2)}) %copy-start.3) | copy-done | bytes 245784
  3.8 0.0 copy-start.4
  3.8 0.9 %copy-done.4 = bf16[6,32,320]{2,1,0:T(8,128)(2,1)S(1)} copy-done((bf16[6,32,320]{2,1,0:T(8,128)(2,1)S(1)}, bf16[6,32,320]{2,1,0:T(8,128)(2,1)}, u32[]{:S(2)}) %copy-start.4) | copy-done | bytes 122904
  4.7 0.0 copy-start.6
  4.7 1.0 %copy-done.6 = bf16[320,640]{1,0:T(8,128)(2,1)S(1)} copy-done((bf16[320,640]{1,0:T(8,128)(2,1)S(1)}, bf16[320,640]{1,0:T(8,128)(2,1)}, u32[]{:S(2)}) %copy-start.6) | copy-done | bytes 409624
  5.7 0.0 copy-start.7
  5.7 0.9 %copy-done.7 = bf16[192,192]{1,0:T(8,128)(2,1)S(1)} copy-done((bf16[192,192]{1,0:T(8,128)(2,1)S(1)}, bf16[192,192]{1,0:T(8,128)(2,1)}, u32[]{:S(2)}) %copy-start.7) | copy-done | bytes 73752
  6.6 0.0 copy-start.10
  6.6 0.7 %copy-done.10 = f32[5,6,32]{2,1,0:T(8,128)S(1)} copy-done((f32[5,6,32]{2,1,0:T(8,128)S(1)}, f32[5,6,32]{2,1,0:T(8,128)}, u32[]{:S(2)}) %copy-start.10) | copy-done | bytes 3864
  7.3 1.8 %project.1.x_ref = bf16[192,1408]{1,0:T(8,128)(2,1)S(1)} custom-call(bf16[192,640]{1,0:T(8,128)(2,1)S(1)} %bitcast.12, bf16[960,640]{1,0:T(8,128)(2,1)S(1)} %bitcast.9, bf16[192,640]{1,0:T(8,128)(2,1)S(1)} %bitcast.14, bf16[320,640]{1,0:T(8,128)(2,1)S(1)} %copy-done.6, bf16[192,320]{1,0:T(8,128)(2,1)S(1)} %bitcast.16, f32[5,6,32]{2,1,0:T(8,128)S(1)} %copy-done.10, ...), custom_call_target="tpu_custom_call" | custom-call | tf_op jit(solution)/shard_map/project/pallas_call | solution.py:534
  9.2 0.0 copy-start.1
  9.2 0.0 copy-start.5
  9.2 0.0 copy-start.8
  9.2 0.0 copy-start.9
  9.2 10.3 %halo.1.near_ref = bf16[816,1408]{1,0:T(8,128)(2,1)S(1)} custom-call(bf16[192,1408]{1,0:T(8,128)(2,1)S(1)} %project.1.x_ref), custom_call_target="tpu_custom_call" | custom-call | tf_op jit(solution)/shard_map/halo/pallas_call | solution.py:541
  19.5 0.0 copy-done.1
  19.5 0.0 copy-done.5
  19.6 0.0 copy-done.8
  19.6 0.0 copy-done.9
  19.6 5.4 %attention.1 = (bf16[192,640]{1,0:T(8,128)(2,1)}, bf16[1280,640]{1,0:T(8,128)(2,1)S(1)}) custom-call(bf16[816,1408]{1,0:T(8,128)(2,1)S(1)} %halo.1.near_ref, bf16[192,816]{1,0:T(8,128)(2,1)S(1)} %copy-done.9, bf16[192,192]{1,0:T(8,128)(2,1)S(1)} %copy-done.8, bf16[192,640]{1,0:T(8,128)(2,1)S(1)} %bitcast.13, bf16[192,640]{1,0:T(8,128)(2,1)S(1)} %bitcast.15, ...), custom_call_target="tpu_custom_call" | custom-call | tf_op jit(solution)/shard_map/attention/pallas_call | solution.py:548
  25.0 40.4 %weight_sums.1 = bf16[2,4,4,40,640]{4,3,2,1,0:T(8,128)(2,1)S(1)} custom-call(bf16[2,4,4,40,640]{4,3,2,1,0:T(8,128)(2,1)S(1)} %bitcast.11), custom_call_target="tpu_custom_call" | custom-call | tf_op jit(solution)/shard_map/weight_sums/pallas_call | solution.py:139
  65.5 1.2 %split.1 = (bf16[960,640]{1,0:T(8,128)(2,1)}, bf16[320,640]{1,0:T(8,128)(2,1)}) custom-call(bf16[1280,640]{1,0:T(8,128)(2,1)S(1)} %bitcast.8), custom_call_target="tpu_custom_call" | custom-call | tf_op jit(solution)/shard_map/split/pallas_call | solution.py:560
Async XLA Ops:
  0.6 1.3 %copy-start = (bf16[640,960]{0,1:T(8,128)(2,1)S(1)}, bf16[640,960]{0,1:T(8,128)(2,1)}, u32[]{:S(2)}) copy-start(bf16[640,960]{0,1:T(8,128)(2,1)} %param.9) | copy-start | bytes 3686404
  1.9 0.9 %copy-start.2 = (bf16[6,32,640]{2,1,0:T(8,128)(2,1)S(1)}, bf16[6,32,640]{2,1,0:T(8,128)(2,1)}, u32[]{:S(2)}) copy-start(bf16[6,32,640]{2,1,0:T(8,128)(2,1)} %param.8) | copy-start | bytes 737284
  2.9 0.9 %copy-start.3 = (bf16[6,32,640]{2,1,0:T(8,128)(2,1)S(1)}, bf16[6,32,640]{2,1,0:T(8,128)(2,1)}, u32[]{:S(2)}) copy-start(bf16[6,32,640]{2,1,0:T(8,128)(2,1)} %param.13) | copy-start | bytes 737284
  3.8 0.9 %copy-start.4 = (bf16[6,32,320]{2,1,0:T(8,128)(2,1)S(1)}, bf16[6,32,320]{2,1,0:T(8,128)(2,1)}, u32[]{:S(2)}) copy-start(bf16[6,32,320]{2,1,0:T(8,128)(2,1)} %param.11) | copy-start | bytes 368644
  4.7 1.0 %copy-start.6 = (bf16[320,640]{1,0:T(8,128)(2,1)S(1)}, bf16[320,640]{1,0:T(8,128)(2,1)}, u32[]{:S(2)}) copy-start(bf16[320,640]{1,0:T(8,128)(2,1)} %wout_ref.1) | copy-start | bytes 1228804
  5.7 0.9 %copy-start.7 = (bf16[192,192]{1,0:T(8,128)(2,1)S(1)}, bf16[192,192]{1,0:T(8,128)(2,1)}, u32[]{:S(2)}) copy-start(bf16[192,192]{1,0:T(8,128)(2,1)} %constant.5.clone.perm_ref) | copy-start | bytes 221188
  6.6 0.7 %copy-start.10 = (f32[5,6,32]{2,1,0:T(8,128)S(1)}, f32[5,6,32]{2,1,0:T(8,128)}, u32[]{:S(2)}) copy-start(f32[5,6,32]{2,1,0:T(8,128)} %norm_ref.1) | copy-start | bytes 11524
  9.2 10.4 %copy-start.1 = (bf16[640,960]{0,1:T(8,128)(2,1)S(1)}, bf16[640,960]{0,1:T(8,128)(2,1)}, u32[]{:S(2)}) copy-start(bf16[640,960]{0,1:T(8,128)(2,1)} %param.9) | copy-start | bytes 3686404
  9.2 10.4 %copy-start.5 = (bf16[6,32,320]{2,1,0:T(8,128)(2,1)S(1)}, bf16[6,32,320]{2,1,0:T(8,128)(2,1)}, u32[]{:S(2)}) copy-start(bf16[6,32,320]{2,1,0:T(8,128)(2,1)} %param.11) | copy-start | bytes 368644
  9.2 10.4 %copy-start.8 = (bf16[192,192]{1,0:T(8,128)(2,1)S(1)}, bf16[192,192]{1,0:T(8,128)(2,1)}, u32[]{:S(2)}) copy-start(bf16[192,192]{1,0:T(8,128)(2,1)} %constant.5.clone.perm_ref) | copy-start | bytes 221188
  9.2 10.4 %copy-start.9 = (bf16[192,816]{1,0:T(8,128)(2,1)S(1)}, bf16[192,816]{1,0:T(8,128)(2,1)}, u32[]{:S(2)}) copy-start(bf16[192,816]{1,0:T(8,128)(2,1)} %constant.4.clone.mask_ref) | copy-start | bytes 940036
